TPU v7x, 256 devices: a whole 4x4x8 slice. The times are simulated.
256 devices in a mesh: dp: 64 (over y, z, core), mp: 4 (over x).
Axes of the slice: x: 4, y: 4, z: 8, core: 2. Of those that a mesh axis runs over, the one named last changes fastest.
Arguments:
- features: bfloat16 [262144, 1024], P('dp', 'mp'), may hold values from -6 to 6
- history: bfloat16 [131072, 1024], P('dp', 'mp'), may hold values from -6 to 6
- adj_values: bfloat16 [2048, 8, 128, 128], P('dp'), may hold values from -0.1875 to 0.1875
- adj_sources: int32 [2048, 8], P('dp'), may hold values from 0 to 191, as said below
- pull_list: int32 [64, 64, 2], P('dp'), may hold values from 0 to 15
- pull_count: int32 [64, 64], P('dp'), may hold values from 0 to 2, as said below
- partner_mask: int32 [1], replicated, may hold values from 1 to 63
- weight: bfloat16 [1024, 1024], P('mp'), may hold values from -0.1875 to 0.1875
- bias: float32 [1024], P('mp'), may hold values from -3 to 3
Outputs:
- layer_out: bfloat16 [262144, 1024], P('dp', 'mp')
Inputs may be any that keep to these rules, and one draw needn't show every extreme that they name: The partner of cluster c is cluster c XOR partner_mask[0]. Slots s >= pull_count[c, o] of pull_list[c, o] are not live; in every draw some owner has all 2 slots live for every cluster. `adj_sources`: indexes sources: own blocks, then partner blocks, then pulled slots; tile 0 of every target block names an own block and tile 1 a partner block. `pull_list`: local block numbers within an owner's history.
All inputs are finite; a program needn't handle non-finite values.
Results may differ from a plain program's by a relative error of at most 0.0045.
Values may be sent and summed in bfloat16 or wider, within the bound.
A program may use at most 128 MiB of HBM per device.

v0:
```python
import jax
import jax.numpy as jnp
from jax import lax
from jax.experimental import pallas as pl
from jax.experimental.pallas import tpu as pltpu
from jax.sharding import Mesh, PartitionSpec as P

NY, NZ, NC = 4, 8, 2
BLK = 128
CHUNKS = 4
DP = ("y", "z", "core")
MESH = pl.DeviceIdType.MESH


def layer_kernel(
    n_mp, src_idx, own, partner, pulled, adj, unread, my_bias, *refs
):
    wts, refs = refs[:n_mp], refs[n_mp:]
    (
        out, srcs, tiles, bias, agg_out, agg_in, res_out,
        load_sem, bias_send, bias_recv, send_a, recv_a, send_b, recv_b,
    ) = refs
    me = lax.axis_index("mp")
    per_chunk, kb = adj.shape[2:4]
    nb, n_pulled = own.shape[0], pulled.shape[0]
    n_src = 2 * nb + n_pulled
    rows = per_chunk * BLK

    def adj_load(q):
        return pltpu.make_async_copy(adj.at[:, q], tiles.at[:, q], load_sem.at[3 + q])

    loads = [
        pltpu.make_async_copy(own, srcs.at[pl.ds(0, nb)], load_sem.at[0]),
        pltpu.make_async_copy(partner, srcs.at[pl.ds(nb, nb)], load_sem.at[1]),
        pltpu.make_async_copy(pulled, srcs.at[pl.ds(2 * nb, n_pulled)], load_sem.at[2]),
    ]
    for load in loads:
        load.start()
    for q in range(CHUNKS):
        adj_load(q).start()
    srcs[n_src] = jnp.zeros(srcs.shape[1:], srcs.dtype)

    barrier = pltpu.get_barrier_semaphore()
    for k in range(1, n_mp):
        pl.semaphore_signal(barrier, inc=1, device_id={"mp": (me + k) % n_mp}, device_id_type=MESH)
    pl.semaphore_wait(barrier, n_mp - 1)

    def to_bias(k):
        return pltpu.make_async_remote_copy(
            src_ref=my_bias,
            dst_ref=bias.at[k],
            send_sem=bias_send.at[k - 1],
            recv_sem=bias_recv.at[k - 1],
            device_id={"mp": (me + k) % n_mp},
            device_id_type=MESH,
        )

    for k in range(1, n_mp):
        to_bias(k).start()
    bias[0] = my_bias[...]
    for load in loads:
        load.wait()
    for k in range(1, n_mp):
        to_bias(k).wait()

    def to_rows(q, k):
        return pltpu.make_async_remote_copy(
            src_ref=agg_out.at[q, k - 1],
            dst_ref=agg_in.at[q, k],
            send_sem=send_a.at[q, k - 1],
            recv_sem=recv_a.at[q, k - 1],
            device_id={"mp": (me + k) % n_mp},
            device_id_type=MESH,
        )

    def to_columns(q, k):
        return pltpu.make_async_remote_copy(
            src_ref=res_out.at[q, k - 1],
            dst_ref=out.at[pl.ds(pl.multiple_of((me * CHUNKS + q) * rows, rows), rows)],
            send_sem=send_b.at[q, k - 1],
            recv_sem=recv_b.at[q, k - 1],
            device_id={"mp": (me + k) % n_mp},
            device_id_type=MESH,
        )

    def aggregate(q, k, dst):
        dev = (me + k) % n_mp

        def one(i, carry):
            first = ((dev * CHUNKS + q) * per_chunk + i) * kb
            lhs = jnp.concatenate([tiles[dev, q, i, j] for j in range(kb)], axis=1)
            rhs = jnp.concatenate([srcs[src_idx[first + j]] for j in range(kb)], axis=0)
            block = jnp.dot(lhs, rhs, preferred_element_type=jnp.float32)
            dst[pl.ds(pl.multiple_of(i * BLK, BLK), BLK), :] = block.astype(dst.dtype)
            return carry

        lax.fori_loop(0, per_chunk, one, 0)

    def multiply(q):
        for k in range(1, n_mp):
            to_rows(q, k).wait_recv()
        for n in list(range(1, n_mp)) + [0]:
            part = bias[(n_mp - n) % n_mp] + jnp.zeros((rows, 1), jnp.float32)
            for k in range(n_mp):
                part = part + jnp.dot(
                    agg_in[q, k], wts[k][(me + n) % n_mp], preferred_element_type=jnp.float32
                )
            part = jnp.maximum(part, 0.0).astype(out.dtype)
            if n:
                res_out[q, n - 1] = part
                to_columns(q, n).start()
            else:
                out[pl.ds(pl.multiple_of((me * CHUNKS + q) * rows, rows), rows), :] = part

    for q in range(CHUNKS + 1):
        if q < CHUNKS:
            adj_load(q).wait()
            for k in (2, 1, 3):
                aggregate(q, k, agg_out.at[q, k - 1])
                to_rows(q, k).start()
            aggregate(q, 0, agg_in.at[q, 0])
        if q:
            multiply(q - 1)
    for q in range(CHUNKS):
        for k in range(1, n_mp):
            to_rows(q, k).wait_send()
            to_columns(q, k).wait()


def layer(src_idx, own, partner, pulled, adj, unread, wts, bias):
    n_mp = len(wts)
    tb, kb = adj.shape[:2]
    adj = adj.reshape(n_mp, CHUNKS, tb // n_mp // CHUNKS, kb, BLK, BLK)
    width = own.shape[-1]
    n_src = own.shape[0] + partner.shape[0] + pulled.shape[0]
    rows = tb // n_mp // CHUNKS * BLK
    any_spec = pl.BlockSpec(memory_space=pl.ANY)
    vmem_spec = pl.BlockSpec(memory_space=pltpu.VMEM)

    def kernel(*refs):
        layer_kernel(n_mp, *refs)

    return pl.pallas_call(
        kernel,
        out_shape=jax.ShapeDtypeStruct((tb * BLK, width), jnp.bfloat16),
        in_specs=[pl.BlockSpec(memory_space=pltpu.SMEM)] + [any_spec] * 5 + [vmem_spec] * (1 + n_mp),
        out_specs=vmem_spec,
        scratch_shapes=[
            pltpu.VMEM((n_src + 1, BLK, width), jnp.bfloat16),
            pltpu.VMEM(adj.shape, jnp.bfloat16),
            pltpu.VMEM((n_mp,) + bias.shape, jnp.float32),
            pltpu.VMEM((CHUNKS, n_mp - 1, rows, width), jnp.bfloat16),
            pltpu.VMEM((CHUNKS, n_mp, rows, width), jnp.bfloat16),
            pltpu.VMEM((CHUNKS, n_mp - 1, rows, width), jnp.bfloat16),
            pltpu.SemaphoreType.DMA((3 + CHUNKS,)),
            pltpu.SemaphoreType.DMA((n_mp - 1,)),
            pltpu.SemaphoreType.DMA((n_mp - 1,)),
        ]
        + [pltpu.SemaphoreType.DMA((CHUNKS, n_mp - 1))] * 4,
        compiler_params=pltpu.CompilerParams(
            collective_id=0, has_side_effects=True, vmem_limit_bytes=44 << 20
        ),
        name="layer",
    )(src_idx, own, partner, pulled, adj, unread, bias, *wts)


def pull_kernel(block_ids, hist, out, *scratch):
    shards = scratch[:NZ]
    picked, load_sem, keep_sem, send_sems, recv_sems = scratch[NZ:]
    y, core = lax.axis_index("y"), lax.axis_index("core")
    cap = picked.shape[2]
    me = y * NC + core
    n_peers = NY * NC - 1

    def peer(n):
        at = 3 * (n + 1) % (NC * NY)
        return (y + at // NC) % NY, (core + at % NC) % NC

    loads = [pltpu.make_async_copy(hist.at[r], shards[r], load_sem.at[r]) for r in range(NZ)]
    for load in loads:
        load.start()
    barrier = pltpu.get_barrier_semaphore()
    for n in range(n_peers):
        to_y, to_core = peer(n)
        pl.semaphore_signal(
            barrier, inc=1, device_id={"y": to_y, "core": to_core}, device_id_type=MESH
        )
    pl.semaphore_wait(barrier, n_peers)

    def rows(r):
        return out.at[pl.ds((me * NZ + r) * cap, cap)]

    def give(r, n):
        to_y, to_core = peer(n)
        return pltpu.make_async_remote_copy(
            src_ref=picked.at[r, n],
            dst_ref=rows(r),
            send_sem=send_sems.at[r, n],
            recv_sem=recv_sems.at[r, n],
            device_id={"y": to_y, "core": to_core},
            device_id_type=MESH,
        )

    def keep(r):
        return pltpu.make_async_copy(picked.at[r, n_peers], rows(r), keep_sem.at[r])

    for r in range(NZ):
        loads[r].wait()

        def one(n, carry):
            to_y, to_core = peer(n)
            first = ((to_y * NC + to_core) * NZ + r) * cap
            for slot in range(cap):
                picked[r, n, slot] = shards[r][block_ids[first + slot]]

            @pl.when(n < n_peers)
            def _():
                give(r, n).start()

            return carry

        lax.fori_loop(0, n_peers + 1, one, 0)
        keep(r).start()

    def finish(r, carry):
        def one(n, inner):
            give(r, n).wait()
            return inner

        lax.fori_loop(0, n_peers, one, 0)
        keep(r).wait()
        return carry

    lax.fori_loop(0, NZ, finish, 0)


def pull(block_ids, hist):
    n_peers = NY * NC
    total = block_ids.shape[0]
    cap = total // n_peers // NZ
    width = hist.shape[-1]
    any_spec = pl.BlockSpec(memory_space=pl.ANY)
    return pl.pallas_call(
        pull_kernel,
        out_shape=jax.ShapeDtypeStruct((total, BLK, width), jnp.bfloat16),
        in_specs=[pl.BlockSpec(memory_space=pltpu.SMEM), any_spec],
        out_specs=any_spec,
        scratch_shapes=[pltpu.VMEM(hist.shape[1:], jnp.bfloat16)] * NZ
        + [
            pltpu.VMEM((NZ, n_peers, cap, BLK, width), jnp.bfloat16),
            pltpu.SemaphoreType.DMA((NZ,)),
            pltpu.SemaphoreType.DMA((NZ,)),
            pltpu.SemaphoreType.DMA((NZ, n_peers - 1)),
            pltpu.SemaphoreType.DMA((NZ, n_peers - 1)),
        ],
        compiler_params=pltpu.CompilerParams(
            collective_id=1, has_side_effects=True, vmem_limit_bytes=60 << 20
        ),
        cost_estimate=pl.CostEstimate(flops=0, bytes_accessed=256 << 20, transcendentals=0),
        name="pull",
    )(block_ids, hist)


def xor_permute(value, axes, size, which):
    def branch(m):
        if m == 0:
            return lambda v: v
        pairs = [(s, s ^ m) for s in range(size)]
        return lambda v: lax.ppermute(v, axes, pairs)

    return lax.switch(which, [branch(m) for m in range(size)], value)


def from_all(value, axis):
    n = lax.axis_size(axis)
    moved = [lax.ppermute(value, axis, [(s, (s + k) % n) for s in range(n)]) for k in range(1, n)]
    return [value] + moved


def per_device(
    features, history, adj_values, adj_sources, pull_list, pull_count, partner_mask, weight, bias
):
    row_count, width = features.shape
    row_blocks = row_count // BLK
    cap = pull_list.shape[-1]
    hist_blocks = history.shape[0] // BLK
    mask = partner_mask[0]
    n_mp = lax.axis_size("mp")
    yc_mask = (mask >> 4) * NC + (mask & 1)
    z_mask = (mask >> 1) & (NZ - 1)

    hist_z = lax.all_gather(history, "z", axis=0, tiled=True)
    wanted = pull_list[0].reshape(NY, NZ, NC, cap).transpose(0, 2, 1, 3).reshape(NY * NC, NZ, cap)
    asked = lax.all_to_all(wanted, ("y", "core"), split_axis=0, concat_axis=0, tiled=True)

    wts = from_all(weight.reshape(width, n_mp, width).transpose(1, 0, 2), "mp")

    half_way = xor_permute(features, ("y", "core"), NY * NC, yc_mask)

    slot_no = jnp.maximum(adj_sources - 2 * row_blocks, 0)
    owner, slot = slot_no // cap, slot_no % cap
    oy, oz, oc = owner // (NZ * NC), (owner // NC) % NZ, owner % NC
    moved = ((oy * NC + oc) * NZ + oz) * cap + slot
    alive = (jnp.arange(cap)[None, :] < pull_count[0][:, None]).reshape(-1)
    n_pulled = NY * NZ * NC * cap
    pulled_src = 2 * row_blocks + jnp.where(alive[slot_no], moved, n_pulled)
    src_idx = jnp.where(adj_sources >= 2 * row_blocks, pulled_src, adj_sources)
    hist_z, half_way, asked, src_idx, *wts = lax.optimization_barrier(
        (hist_z, half_way, asked.reshape(-1), src_idx.reshape(-1), *wts)
    )

    def pull_beside(m):
        def branch(rows, ids, hist):
            if m:
                rows = lax.ppermute(rows, "z", [(s, s ^ m) for s in range(NZ)])
            return rows, pull(ids, hist)

        return branch

    partner_rows, pulled = lax.switch(
        z_mask,
        [pull_beside(m) for m in range(NZ)],
        half_way,
        asked,
        hist_z.reshape(NZ, hist_blocks, BLK, width),
    )

    return layer(
        src_idx,
        features.reshape(row_blocks, BLK, width),
        partner_rows.reshape(row_blocks, BLK, width),
        pulled,
        adj_values,
        half_way,
        wts,
        bias.reshape(1, width),
    )


def solution(mesh):
    n_mp = mesh.devices.shape[1]
    fine = Mesh(mesh.devices.reshape(NY, NZ, NC, n_mp), ("y", "z", "core", "mp"))
    in_specs = (
        P(DP, "mp"),
        P(DP, "mp"),
        P(DP, None, None, None),
        P(DP, None),
        P(DP, None, None),
        P(DP, None),
        P(),
        P("mp", None),
        P("mp"),
    )
    return jax.shard_map(
        per_device, mesh=fine, in_specs=in_specs, out_specs=P(DP, "mp"), check_vma=False
    )
```

profile of v0, /device:TPU:1, one launch (start us, length us, event | category | flops | bytes accessed | tf_op | source)
XLA Modules:
  0.0 269.6 jit_solution(13240759509330589914)
XLA Ops:
  6.5 0.7 all-gather.2.cloned.1.call-update
  7.3 1.2 copy.25
  8.5 0.2 copy.26
  8.7 3.4 %collective-permute-start.16 = (bf16[4,256,256]{2,1,0:T(8,128)(2,1)S(1)}, bf16[4,256,256]{2,1,0:T(8,128)(2,1)S(1)}, u32[]{:S(2)}, u32[]{:S(2)}) collective-permute-start(bf16[4,256,256]{2,1,0:T(8,128)(2,1)S(1)} %bitcast.14), channel_id=1, source_target_pairs={{0,3},{1,0},{2,1},{3,2},{4,7},{5,4},{6,5},{7,6},{8,11},{9,8},{10,9... | collective-permute-start | bytes 1572872 | tf_op jit(solution)/shard_map/ppermute | solution.py:276
  12.1 0.5 collective-permute-start.15
  12.6 0.6 collective-permute-start.14
  13.2 0.1 reshape_squeeze.3
  13.3 0.1 copy.19
  13.5 0.6 copy.20
  14.1 6.0 %all-to-all-start = ((s32[8,8,2]{1,2,0:T(2,128)}), s32[8,8,2]{1,2,0:T(2,128)S(1)}, u32[]{:S(2)}, u32[]{:S(2)}) async-start(s32[8,8,2]{1,2,0:T(2,128)} %copy.20), calls=%async_computation | async-start | bytes 16384 | tf_op jit(solution)/shard_map/all_to_all | solution.py:294
  20.8 0.2 lt.38
  21.1 1.9 gather_fusion
  23.0 0.1 reshape.59
  23.3 49.2 %conditional.2 = (bf16[4096,256]{1,0:T(8,128)(2,1)}) conditional(s32[]{:T(128)} %bitcast, bf16[4096,256]{1,0:T(8,128)(2,1)} %param.25, bf16[4096,256]{1,0:T(8,128)(2,1)} %param.25, bf16[4096,256]{1,0:T(8,128)(2,1)} %param.25, bf16[4096,256]{1,0:T(8,128)(2,1)} %param.25, bf16[4096,256]{1,0:T(8,128)(2,1)} %param.25, ...), branch_computations={%region_0.0_spmd, %region_1.0_spmd, %region_2.0_spmd, %region_3.0_... | conditional | bytes 8388656 | solution.py:271
  23.3 3.0 %collective-permute-start.3 = (bf16[4096,256]{1,0:T(8,128)(2,1)}, bf16[4096,256]{1,0:T(8,128)(2,1)}, u32[]{:S(2)}, u32[]{:S(2)}) collective-permute-start(bf16[4096,256]{1,0:T(8,128)(2,1)} %param.4), channel_id=1, source_target_pairs={{0,128},{4,132},{64,192},{68,196},{128,0},{132,4},{192,64},{196,68... | collective-permute-start | bytes 6291464 | tf_op jit(solution)/shard_map/cond/branch_4_fun/ppermute | solution.py:269
  26.3 46.2 %collective-permute-done.3 = bf16[4096,256]{1,0:T(8,128)(2,1)} collective-permute-done((bf16[4096,256]{1,0:T(8,128)(2,1)}, bf16[4096,256]{1,0:T(8,128)(2,1)}, u32[]{:S(2)}, u32[]{:S(2)}) %collective-permute-start.3) | collective-permute-done | bytes 2097184 | tf_op jit(solution)/shard_map/cond/branch_4_fun/ppermute | solution.py:269
  72.5 0.1 copy.21
  72.6 0.1 reshape.50
  72.8 34.3 %all-gather.2.cloned.1.call-done = bf16[16384,256]{1,0:T(8,128)(2,1)} async-done(((bf16[2048,256]{1,0:T(8,128)(2,1)}), bf16[16384,256]{1,0:T(8,128)(2,1)}) %all-gather.2.cloned.1.call-update) | async-done | bytes 8388624 | tf_op jit(solution)/shard_map/all_gather | solution.py:292
  107.1 98.5 %conditional.3 = (bf16[4096,256]{1,0:T(8,128)(2,1)}, bf16[128,128,256]{2,1,0:T(8,128)(2,1)}) conditional(s32[]{:T(128)} %bitcast.7, (s32[128]{0:T(128)S(1)}, bf16[8,16,128,256]{3,2,1,0:T(8,128)(2,1)}, bf16[4096,256]{1,0:T(8,128)(2,1)}) %tuple.83, (bf16[4096,256]{1,0:T(8,128)(2,1)}, s32[128]{0:T(128)S(1)}, ...), branch_computations={%region_8.9_spmd, %region_9.10_spmd, %region_10.11_spmd, %region_1... | conditional | bytes 276824128 | solution.py:320
  107.1 0.5 collective-permute-start.8
  107.6 97.9 %pull.10 = bf16[128,128,256]{2,1,0:T(8,128)(2,1)} custom-call(s32[128]{0:T(128)S(1)} %get-tuple-element.77.block_ids, bf16[8,16,128,256]{3,2,1,0:T(8,128)(2,1)} %get-tuple-element.78.hist), custom_call_target="tpu_custom_call" | custom-call | bytes 268435456 | tf_op jit(solution)/shard_map/cond/branch_2_fun/pull/pallas_call | solution.py:243
  205.7 55.7 %layer.1 = bf16[4096,256]{1,0:T(8,128)(2,1)S(1)} custom-call(s32[256]{0:T(256)S(1)} %reshape.51.refs_0_, bf16[32,128,256]{2,1,0:T(8,128)(2,1)} %bitcast.28, bf16[32,128,256]{2,1,0:T(8,128)(2,1)} %bitcast.9.refs_2_, bf16[128,128,256]{2,1,0:T(8,128)(2,1)} %get-tuple-element.109.refs_3_, bf16[4,4,2,8,128,128]{5,4,3,2,1,0:T(8,128)(2,1)} %bitcast.27, ...), custom_call_target="tpu_custom_call" | custom-call | tf_op jit(solution)/shard_map/layer/pallas_call | solution.py:143
  261.4 1.3 copy.53
  (21 shorter events, 0.4 us)
Async XLA Ops:
  6.5 6.7 %copy-start.2 = (s32[1,64,2]{1,2,0:T(2,128)S(1)}, s32[1,64,2]{1,2,0:T(2,128)}, u32[]{:S(2)}) copy-start(s32[1,64,2]{1,2,0:T(2,128)} %param.29) | copy-start | bytes 1540
  6.5 14.2 %copy-start.3 = (s32[1,64]{1,0:T(1,128)S(1)}, s32[1,64]{1,0:T(1,128)}, u32[]{:S(2)}) copy-start(s32[1,64]{1,0:T(1,128)} %param.30) | copy-start | bytes 772
  6.5 14.4 %copy-start.1 = (s32[32,8]{0,1:T(8,128)S(1)}, s32[32,8]{0,1:T(8,128)}, u32[]{:S(2)}) copy-start(s32[32,8]{0,1:T(8,128)} %param.28) | copy-start | bytes 3076
  6.5 100.6 %all-gather.2.cloned.1.call-start = ((), (), s32[]{:S(2)}) async-start(), calls=%async_computation.1 | async-start | bytes 9437184 | tf_op jit(solution)/shard_map/all_gather | solution.py:292
  8.7 64.0 %collective-permute-start.16 = (bf16[4,256,256]{2,1,0:T(8,128)(2,1)S(1)}, bf16[4,256,256]{2,1,0:T(8,128)(2,1)S(1)}, u32[]{:S(2)}, u32[]{:S(2)}) collective-permute-start(bf16[4,256,256]{2,1,0:T(8,128)(2,1)S(1)} %bitcast.14), channel_id=1, source_target_pairs={{0,3},{1,0},{2,1},{3,2},{4,7},{5,4},{6,5},{7,6},{8,11},{9,8},{10,9... | collective-permute-start | bytes 1572872 | tf_op jit(solution)/shard_map/ppermute | solution.py:276
  12.1 60.7 %collective-permute-start.15 = (bf16[4,256,256]{2,1,0:T(8,128)(2,1)S(1)}, bf16[4,256,256]{2,1,0:T(8,128)(2,1)S(1)}, u32[]{:S(2)}, u32[]{:S(2)}) collective-permute-start(bf16[4,256,256]{2,1,0:T(8,128)(2,1)S(1)} %bitcast.15), channel_id=1, source_target_pairs={{0,2},{1,3},{2,0},{3,1},{4,6},{5,7},{6,4},{7,5},{8,10},{9,11},{10,... | collective-permute-start | bytes 1572872 | tf_op jit(solution)/shard_map/ppermute | solution.py:276
  12.6 60.1 %collective-permute-start.14 = (bf16[4,256,256]{2,1,0:T(8,128)(2,1)S(1)}, bf16[4,256,256]{2,1,0:T(8,128)(2,1)S(1)}, u32[]{:S(2)}, u32[]{:S(2)}) collective-permute-start(bf16[4,256,256]{2,1,0:T(8,128)(2,1)S(1)} %bitcast.16), channel_id=1, source_target_pairs={{0,1},{1,2},{2,3},{3,0},{4,5},{5,6},{6,7},{7,4},{8,9},{9,10},{10,1... | collective-permute-start | bytes 1572872 | tf_op jit(solution)/shard_map/ppermute | solution.py:276
  14.1 58.4 %all-to-all-start = ((s32[8,8,2]{1,2,0:T(2,128)}), s32[8,8,2]{1,2,0:T(2,128)S(1)}, u32[]{:S(2)}, u32[]{:S(2)}) async-start(s32[8,8,2]{1,2,0:T(2,128)} %copy.20), calls=%async_computation | async-start | bytes 16384 | tf_op jit(solution)/shard_map/all_to_all | solution.py:294
  23.3 49.2 %collective-permute-start.3 = (bf16[4096,256]{1,0:T(8,128)(2,1)}, bf16[4096,256]{1,0:T(8,128)(2,1)}, u32[]{:S(2)}, u32[]{:S(2)}) collective-permute-start(bf16[4096,256]{1,0:T(8,128)(2,1)} %param.4), channel_id=1, source_target_pairs={{0,128},{4,132},{64,192},{68,196},{128,0},{132,4},{192,64},{196,68... | collective-permute-start | bytes 6291464 | tf_op jit(solution)/shard_map/cond/branch_4_fun/ppermute | solution.py:269
  107.1 98.6 %copy-start = (f32[256]{0:T(256)S(1)}, f32[256]{0:T(256)}, u32[]{:S(2)}) copy-start(f32[256]{0:T(256)} %param.33) | copy-start | bytes 3076
  107.1 98.4 %collective-permute-start.8 = (bf16[4096,256]{1,0:T(8,128)(2,1)}, bf16[4096,256]{1,0:T(8,128)(2,1)}, u32[]{:S(2)}, u32[]{:S(2)}) collective-permute-start(bf16[4096,256]{1,0:T(8,128)(2,1)} %get-tuple-element.76), channel_id=1, source_target_pairs={{0,16},{8,24},{16,0},{24,8},{32,48},{40,56},{48,32},{56,40},{1,17}... | collective-permute-start | bytes 6291464 | tf_op jit(solution)/shard_map/cond/branch_2_fun/ppermute | solution.py:315
Sparse Core Ops, SparseCore 0:
  9.2 97.9 all-gather.1
where the time goes:
time: 270 us
  Pallas kernels  154 us (57%)
  waiting for transfers between devices  81.3 us (30%)
  between operations  14.2 us (5%)
  starting transfers between devices  13.9 us (5%)
  local copies, waits for them, and re-layouts  6.24 us (2%)
    pallas_call x1, Pallas kernels, pull(): pl.pallas_call(pull_kernel, out_shape=jax.ShapeDtypeStruct((total, BLK, w...  97.9 us
    pallas_call x1, Pallas kernels, layer(): pl.pallas_call(kernel, out_shape=jax.ShapeDtypeStruct((tb * BLK, width),...  55.7 us
    ppermute x1, waiting for transfers between devices, branch(): return lambda v: lax.ppermute(v, axes, pairs)  46.2 us
    all_gather x1, waiting for transfers between devices, per_device(): hist_z = lax.all_gather(history, 'z', axis=0, tiled=True)  34.3 us
    all_to_all x1, starting transfers between devices, per_device(): lax.all_to_all(wanted, ('y', 'core'), split_axis=0, concat_axis=0, tiled=...  5.98 us
  transfers between devices with their start and end apart: 7, of which 2 were waited for; matrix products, arithmetic and copies ran while one was open for 2% of the time, Pallas kernels for 36%

commit v1 on v0

--- a/solution.py
+++ b/solution.py
@@ -8,22 +8,23 @@
 NY, NZ, NC = 4, 8, 2
 BLK = 128
 CHUNKS = 4
+Z_PIECES = 4
+Z_AHEAD = 2
+Y_PIECES = 4
 DP = ("y", "z", "core")
 MESH = pl.DeviceIdType.MESH
 
 
 def layer_kernel(
-    n_mp, src_idx, own, partner, pulled, adj, unread, my_bias, *refs
+    n_mp, src_no, counts, own, partner, pulled, adj, unread, w_rows, my_bias,
+    out, srcs, tiles, wts, bias, agg_out, agg_in, res_out,
+    load_sem, w_sem, bias_send, bias_recv, send_a, recv_a, send_b, recv_b,
 ):
-    wts, refs = refs[:n_mp], refs[n_mp:]
-    (
-        out, srcs, tiles, bias, agg_out, agg_in, res_out,
-        load_sem, bias_send, bias_recv, send_a, recv_a, send_b, recv_b,
-    ) = refs
     me = lax.axis_index("mp")
     per_chunk, kb = adj.shape[2:4]
     nb, n_pulled = own.shape[0], pulled.shape[0]
     n_src = 2 * nb + n_pulled
+    cap = n_pulled // (NY * NZ * NC)
     rows = per_chunk * BLK
 
     def adj_load(q):
@@ -38,6 +39,16 @@
         load.start()
     for q in range(CHUNKS):
         adj_load(q).start()
+    cols = own.shape[-1]
+    w_loads = [
+        pltpu.make_async_copy(
+            w_rows.at[k, :, pl.ds(n * cols, cols)], wts.at[k, n], w_sem.at[k, n]
+        )
+        for k in range(n_mp)
+        for n in range(n_mp)
+    ]
+    for load in w_loads:
+        load.start()
     srcs[n_src] = jnp.zeros(srcs.shape[1:], srcs.dtype)
 
     barrier = pltpu.get_barrier_semaphore()
@@ -83,13 +94,21 @@
             device_id_type=MESH,
         )
 
+    def place(src):
+        at = jnp.maximum(src - 2 * nb, 0)
+        owner, slot = at // cap, at % cap
+        oy, oz, oc = owner // (NZ * NC), owner // NC % NZ, owner % NC
+        moved = 2 * nb + ((oy * NC + oc) * NZ + oz) * cap + slot
+        moved = jnp.where(slot < counts[owner], moved, n_src)
+        return jnp.where(src < 2 * nb, src, moved)
+
     def aggregate(q, k, dst):
         dev = (me + k) % n_mp
 
         def one(i, carry):
             first = ((dev * CHUNKS + q) * per_chunk + i) * kb
             lhs = jnp.concatenate([tiles[dev, q, i, j] for j in range(kb)], axis=1)
-            rhs = jnp.concatenate([srcs[src_idx[first + j]] for j in range(kb)], axis=0)
+            rhs = jnp.concatenate([srcs[place(src_no[first + j])] for j in range(kb)], axis=0)
             block = jnp.dot(lhs, rhs, preferred_element_type=jnp.float32)
             dst[pl.ds(pl.multiple_of(i * BLK, BLK), BLK), :] = block.astype(dst.dtype)
             return carry
@@ -103,7 +122,7 @@
             part = bias[(n_mp - n) % n_mp] + jnp.zeros((rows, 1), jnp.float32)
             for k in range(n_mp):
                 part = part + jnp.dot(
-                    agg_in[q, k], wts[k][(me + n) % n_mp], preferred_element_type=jnp.float32
+                    agg_in[q, k], wts[k, (me + n) % n_mp], preferred_element_type=jnp.float32
                 )
             part = jnp.maximum(part, 0.0).astype(out.dtype)
             if n:
@@ -119,6 +138,9 @@
                 aggregate(q, k, agg_out.at[q, k - 1])
                 to_rows(q, k).start()
             aggregate(q, 0, agg_in.at[q, 0])
+        if q == 1:
+            for load in w_loads:
+                load.wait()
         if q:
             multiply(q - 1)
     for q in range(CHUNKS):
@@ -127,8 +149,8 @@
             to_columns(q, k).wait()
 
 
-def layer(src_idx, own, partner, pulled, adj, unread, wts, bias):
-    n_mp = len(wts)
+def layer(src_no, counts, own, partner, pulled, adj, unread, wts, bias):
+    n_mp = wts.shape[0]
     tb, kb = adj.shape[:2]
     adj = adj.reshape(n_mp, CHUNKS, tb // n_mp // CHUNKS, kb, BLK, BLK)
     width = own.shape[-1]
@@ -143,25 +165,195 @@
     return pl.pallas_call(
         kernel,
         out_shape=jax.ShapeDtypeStruct((tb * BLK, width), jnp.bfloat16),
-        in_specs=[pl.BlockSpec(memory_space=pltpu.SMEM)] + [any_spec] * 5 + [vmem_spec] * (1 + n_mp),
+        in_specs=[pl.BlockSpec(memory_space=pltpu.SMEM)] * 2 + [any_spec] * 6 + [vmem_spec],
         out_specs=vmem_spec,
         scratch_shapes=[
             pltpu.VMEM((n_src + 1, BLK, width), jnp.bfloat16),
             pltpu.VMEM(adj.shape, jnp.bfloat16),
+            pltpu.VMEM((n_mp, n_mp, width, width), jnp.bfloat16),
             pltpu.VMEM((n_mp,) + bias.shape, jnp.float32),
             pltpu.VMEM((CHUNKS, n_mp - 1, rows, width), jnp.bfloat16),
             pltpu.VMEM((CHUNKS, n_mp, rows, width), jnp.bfloat16),
             pltpu.VMEM((CHUNKS, n_mp - 1, rows, width), jnp.bfloat16),
             pltpu.SemaphoreType.DMA((3 + CHUNKS,)),
+            pltpu.SemaphoreType.DMA((n_mp, n_mp)),
             pltpu.SemaphoreType.DMA((n_mp - 1,)),
             pltpu.SemaphoreType.DMA((n_mp - 1,)),
         ]
         + [pltpu.SemaphoreType.DMA((CHUNKS, n_mp - 1))] * 4,
         compiler_params=pltpu.CompilerParams(
-            collective_id=0, has_side_effects=True, vmem_limit_bytes=44 << 20
+            collective_id=0, has_side_effects=True, vmem_limit_bytes=60 << 20
         ),
         name="layer",
-    )(src_idx, own, partner, pulled, adj, unread, bias, *wts)
+    )(src_no, counts, own, partner, pulled, adj, unread, wts, bias)
+
+
+def spread_kernel(
+    hist, feat, asks, weight, hist_z, feat_y, asked, wts,
+    hist_v, feat_v, weight_v, in_sem, own_sem,
+    z_send, z_recv, y_send, y_recv, ask_send, ask_recv, w_send, w_recv,
+):
+    y, z, core, mp = (lax.axis_index(name) for name in ("y", "z", "core", "mp"))
+    n_mp = wts.shape[0]
+    z_piece = hist.shape[0] // Z_PIECES
+    n_peers = NY * NC - 1
+
+    def peer(n):
+        at = n + 1
+        return (y + at // NC) % NY, (core + at % NC) % NC
+
+    loads = [
+        pltpu.make_async_copy(hist, hist_v, in_sem.at[0]),
+        pltpu.make_async_copy(feat, feat_v, in_sem.at[1]),
+        pltpu.make_async_copy(weight, weight_v, in_sem.at[2]),
+    ]
+    own = [
+        pltpu.make_async_copy(hist_v, hist_z.at[z], own_sem.at[0]),
+        pltpu.make_async_copy(feat_v, feat_y.at[y], own_sem.at[1]),
+        pltpu.make_async_copy(weight_v, wts.at[0], own_sem.at[2]),
+        pltpu.make_async_copy(asks, asked.at[y * NC + core], own_sem.at[3]),
+    ]
+    for load in loads:
+        load.start()
+
+    barrier = pltpu.get_barrier_semaphore()
+    for n in range(n_peers):
+        to_y, to_core = peer(n)
+        pl.semaphore_signal(
+            barrier, inc=1, device_id={"y": to_y, "core": to_core}, device_id_type=MESH
+        )
+    for dz in (1, NZ - 1):
+        pl.semaphore_signal(barrier, inc=1, device_id={"z": (z + dz) % NZ}, device_id_type=MESH)
+    for k in range(1, n_mp):
+        pl.semaphore_signal(barrier, inc=1, device_id={"mp": (mp + k) % n_mp}, device_id_type=MESH)
+    pl.semaphore_wait(barrier, n_peers + 2 + n_mp - 1)
+
+    def z_hop(up, s, p):
+        at = (z + (1 - s if up else s - 1)) % NZ
+        part = pl.ds(p * z_piece, z_piece)
+        return pltpu.make_async_remote_copy(
+            src_ref=(hist if s == 1 else hist_z.at[at]).at[part],
+            dst_ref=hist_z.at[at, part],
+            send_sem=z_send.at[0 if up else 1, s - 1, p],
+            recv_sem=z_recv.at[0 if up else 1, s - 1, p],
+            device_id={"z": (z + (1 if up else NZ - 1)) % NZ},
+            device_id_type=MESH,
+        )
+
+    def y_hop(up, s, p):
+        at = (y + (1 - s if up else s - 1)) % NY
+        return pltpu.make_async_remote_copy(
+            src_ref=(feat if s == 1 else feat_y.at[at]).at[p],
+            dst_ref=feat_y.at[at, p],
+            send_sem=y_send.at[0 if up else 1, s - 1, p],
+            recv_sem=y_recv.at[0 if up else 1, s - 1, p],
+            device_id={"y": (y + (1 if up else NY - 1)) % NY},
+            device_id_type=MESH,
+        )
+
+    def order(size, pieces, up):
+        last = range(pieces // 2) if up else range(pieces // 2, pieces)
+        return [(up, s, p) for s in range(1, size // 2) for p in range(pieces)] + [
+            (up, size // 2, p) for p in last
+        ]
+
+    def ask(n):
+        to_y, to_core = peer(n)
+        return pltpu.make_async_remote_copy(
+            src_ref=asks,
+            dst_ref=asked.at[y * NC + core],
+            send_sem=ask_send.at[n],
+            recv_sem=ask_recv.at[n],
+            device_id={"y": to_y, "core": to_core},
+            device_id_type=MESH,
+        )
+
+    def share(k):
+        return pltpu.make_async_remote_copy(
+            src_ref=weight,
+            dst_ref=wts.at[k],
+            send_sem=w_send.at[k - 1],
+            recv_sem=w_recv.at[k - 1],
+            device_id={"mp": (mp + k) % n_mp},
+            device_id_type=MESH,
+        )
+
+    z_ways = [order(NZ, Z_PIECES, up) for up in (True, False)]
+    y_ways = [order(NY, Y_PIECES, up) for up in (True, False)]
+    for way in z_ways:
+        for hop in way[:Z_AHEAD]:
+            z_hop(*hop).start()
+    for way in y_ways:
+        for hop in way[:Y_PIECES]:
+            y_hop(*hop).start()
+    for n in range(n_peers):
+        ask(n).start()
+    for k in range(1, n_mp):
+        share(k).start()
+    for load in loads:
+        load.wait()
+    for copy in own:
+        copy.start()
+
+    for i in range(Z_AHEAD, len(z_ways[0])):
+        for way in z_ways:
+            up, s, p = way[i]
+            z_hop(*way[i - Z_AHEAD]).wait_send()
+            if s > 1:
+                z_hop(up, s - 1, p).wait_recv()
+            z_hop(up, s, p).start()
+        if i == len(z_ways[0]) * 3 // 4:
+            for way in y_ways:
+                for up, s, p in way[Y_PIECES:]:
+                    y_hop(up, s - 1, p).wait_recv()
+                    y_hop(up, s, p).start()
+    for make, ways, ahead in ((z_hop, z_ways, Z_AHEAD), (y_hop, y_ways, len(y_ways[0]))):
+        for way in ways:
+            for up, s, p in way:
+                if (up, s + 1, p) not in way:
+                    make(up, s, p).wait_recv()
+            for hop in way[-ahead:]:
+                make(*hop).wait_send()
+    for n in range(n_peers):
+        ask(n).wait()
+    for k in range(1, n_mp):
+        share(k).wait()
+    for copy in own:
+        copy.wait()
+
+
+def spread(history, features, asks, weight, n_mp):
+    any_spec = pl.BlockSpec(memory_space=pl.ANY)
+    n_peers = NY * NC - 1
+
+    def out(lead, value):
+        return jax.ShapeDtypeStruct((lead,) + value.shape, value.dtype)
+
+    return pl.pallas_call(
+        spread_kernel,
+        out_shape=(out(NZ, history), out(NY, features), out(NY * NC, asks), out(n_mp, weight)),
+        in_specs=[any_spec] * 4,
+        out_specs=(any_spec,) * 4,
+        scratch_shapes=[
+            pltpu.VMEM(history.shape, history.dtype),
+            pltpu.VMEM(features.shape, features.dtype),
+            pltpu.VMEM(weight.shape, weight.dtype),
+            pltpu.SemaphoreType.DMA((3,)),
+            pltpu.SemaphoreType.DMA((4,)),
+            pltpu.SemaphoreType.DMA((2, NZ // 2, Z_PIECES)),
+            pltpu.SemaphoreType.DMA((2, NZ // 2, Z_PIECES)),
+            pltpu.SemaphoreType.DMA((2, NY // 2, Y_PIECES)),
+            pltpu.SemaphoreType.DMA((2, NY // 2, Y_PIECES)),
+            pltpu.SemaphoreType.DMA((n_peers,)),
+            pltpu.SemaphoreType.DMA((n_peers,)),
+            pltpu.SemaphoreType.DMA((n_mp - 1,)),
+            pltpu.SemaphoreType.DMA((n_mp - 1,)),
+        ],
+        compiler_params=pltpu.CompilerParams(
+            collective_id=2, has_side_effects=True, vmem_limit_bytes=60 << 20
+        ),
+        name="spread",
+    )(history, features, asks, weight)
 
 
 def pull_kernel(block_ids, hist, out, *scratch):
@@ -171,6 +363,7 @@
     cap = picked.shape[2]
     me = y * NC + core
     n_peers = NY * NC - 1
+    per_ask = NY * NZ * NC * cap
 
     def peer(n):
         at = 3 * (n + 1) % (NC * NY)
@@ -209,7 +402,7 @@
 
         def one(n, carry):
             to_y, to_core = peer(n)
-            first = ((to_y * NC + to_core) * NZ + r) * cap
+            first = (to_y * NC + to_core) * per_ask + ((y * NZ + r) * NC + core) * cap
             for slot in range(cap):
                 picked[r, n, slot] = shards[r][block_ids[first + slot]]
 
@@ -236,7 +429,7 @@
 
 def pull(block_ids, hist):
     n_peers = NY * NC
-    total = block_ids.shape[0]
+    total = block_ids.shape[0] // n_peers
     cap = total // n_peers // NZ
     width = hist.shape[-1]
     any_spec = pl.BlockSpec(memory_space=pl.ANY)
@@ -261,72 +454,46 @@
     )(block_ids, hist)
 
 
-def xor_permute(value, axes, size, which):
-    def branch(m):
-        if m == 0:
-            return lambda v: v
-        pairs = [(s, s ^ m) for s in range(size)]
-        return lambda v: lax.ppermute(v, axes, pairs)
-
-    return lax.switch(which, [branch(m) for m in range(size)], value)
-
-
-def from_all(value, axis):
-    n = lax.axis_size(axis)
-    moved = [lax.ppermute(value, axis, [(s, (s + k) % n) for s in range(n)]) for k in range(1, n)]
-    return [value] + moved
-
-
 def per_device(
     features, history, adj_values, adj_sources, pull_list, pull_count, partner_mask, weight, bias
 ):
     row_count, width = features.shape
     row_blocks = row_count // BLK
-    cap = pull_list.shape[-1]
     hist_blocks = history.shape[0] // BLK
     mask = partner_mask[0]
     n_mp = lax.axis_size("mp")
-    yc_mask = (mask >> 4) * NC + (mask & 1)
-    z_mask = (mask >> 1) & (NZ - 1)
-
-    hist_z = lax.all_gather(history, "z", axis=0, tiled=True)
-    wanted = pull_list[0].reshape(NY, NZ, NC, cap).transpose(0, 2, 1, 3).reshape(NY * NC, NZ, cap)
-    asked = lax.all_to_all(wanted, ("y", "core"), split_axis=0, concat_axis=0, tiled=True)
-
-    wts = from_all(weight.reshape(width, n_mp, width).transpose(1, 0, 2), "mp")
-
-    half_way = xor_permute(features, ("y", "core"), NY * NC, yc_mask)
-
-    slot_no = jnp.maximum(adj_sources - 2 * row_blocks, 0)
-    owner, slot = slot_no // cap, slot_no % cap
-    oy, oz, oc = owner // (NZ * NC), (owner // NC) % NZ, owner % NC
-    moved = ((oy * NC + oc) * NZ + oz) * cap + slot
-    alive = (jnp.arange(cap)[None, :] < pull_count[0][:, None]).reshape(-1)
-    n_pulled = NY * NZ * NC * cap
-    pulled_src = 2 * row_blocks + jnp.where(alive[slot_no], moved, n_pulled)
-    src_idx = jnp.where(adj_sources >= 2 * row_blocks, pulled_src, adj_sources)
-    hist_z, half_way, asked, src_idx, *wts = lax.optimization_barrier(
-        (hist_z, half_way, asked.reshape(-1), src_idx.reshape(-1), *wts)
+    y_mask = mask >> 4
+    zc_mask = mask & (NZ * NC - 1)
+
+    hist_z, feat_y, asked, wts = spread(
+        history.reshape(hist_blocks, BLK, width),
+        features.reshape(Y_PIECES, row_count // Y_PIECES, width),
+        pull_list.reshape(1, -1),
+        weight,
+        n_mp,
     )
+
+    half_way = lax.dynamic_index_in_dim(feat_y, lax.axis_index("y") ^ y_mask, keepdims=False)
 
     def pull_beside(m):
         def branch(rows, ids, hist):
             if m:
-                rows = lax.ppermute(rows, "z", [(s, s ^ m) for s in range(NZ)])
+                rows = lax.ppermute(rows, ("z", "core"), [(s, s ^ m) for s in range(NZ * NC)])
             return rows, pull(ids, hist)
 
         return branch
 
     partner_rows, pulled = lax.switch(
-        z_mask,
-        [pull_beside(m) for m in range(NZ)],
+        zc_mask,
+        [pull_beside(m) for m in range(NZ * NC)],
         half_way,
-        asked,
-        hist_z.reshape(NZ, hist_blocks, BLK, width),
+        asked.reshape(-1),
+        hist_z,
     )
 
     return layer(
-        src_idx,
+        adj_sources.reshape(-1),
+        pull_count.reshape(-1),
         features.reshape(row_blocks, BLK, width),
         partner_rows.reshape(row_blocks, BLK, width),
         pulled,

time: 270 us -> 254 us (0.941)
  Pallas kernels: 154 us -> 245 us
  waiting for transfers between devices: 81.3 us -> 0.01 us
  between operations: 14.2 us -> 0.71 us
  starting transfers between devices: 13.9 us -> 0.96 us
    pallas_call x0 -> x1, Pallas kernels: none -> 90.8 us  [spread(): pl.pallas_call(spread_kernel, out_shape=(out(NZ, history), out(NY, featur...]
    ppermute x5 -> x1, waiting for transfers between devices: 46.2 us -> 0.01 us  [branch(): lax.ppermute(rows, ('z', 'core'), [(s, s ^ m) for s in range(NZ * NC)])]
    all_gather x1 -> x0, waiting for transfers between devices: 34.3 us -> none  [per_device(): hist_z = lax.all_gather(history, 'z', axis=0, tiled=True)]
    ppermute x5 -> x1, starting transfers between devices: 7.95 us -> 0.96 us  [branch(): lax.ppermute(rows, ('z', 'core'), [(s, s ^ m) for s in range(NZ * NC)])]
    all_to_all x1 -> x0, starting transfers between devices: 5.98 us -> none  [per_device(): lax.all_to_all(wanted, ('y', 'core'), split_axis=0, concat_axis=0, tiled=...]
  transfers between devices with their start and end apart: 7 -> 1, of which waited for: 2 -> 0; matrix products, arithmetic and copies ran while one was open for 2% -> 0% of each run, Pallas kernels for 36% -> 38%
where the time goes in v1:
time: 254 us
  Pallas kernels  245 us (96%)
  local copies, waits for them, and re-layouts  6.94 us (3%)
    pallas_call x1, Pallas kernels, pull(): pl.pallas_call(pull_kernel, out_shape=jax.ShapeDtypeStruct((total, BLK, w...  96.7 us
    pallas_call x1, Pallas kernels, spread(): pl.pallas_call(spread_kernel, out_shape=(out(NZ, history), out(NY, featur...  90.8 us
    pallas_call x1, Pallas kernels, layer(): pl.pallas_call(kernel, out_shape=jax.ShapeDtypeStruct((tb * BLK, width),...  57.8 us
  transfers between devices with their start and end apart: 1, of which 0 were waited for; matrix products, arithmetic and copies ran while one was open for 0% of the time, Pallas kernels for 38%

profile of v1, /device:TPU:1, one launch (start us, length us, event | category | flops | bytes accessed | tf_op | source)
XLA Modules:
  0.0 254.3 jit_solution(4282688131882362047)
XLA Ops:
  0.7 0.8 copy.12
  1.4 0.7 reshape.42.asks
  2.1 90.8 %spread.1 = (bf16[8,16,128,256]{3,2,1,0:T(8,128)(2,1)}, bf16[4,4,1024,256]{3,2,1,0:T(8,128)(2,1)}, s32[8,1,128]{2,1,0:T(1,128)S(1)}, bf16[4,256,1024]{2,1,0:T(8,128)(2,1)}) custom-call(bf16[16,128,256]{2,1,0:T(8,128)(2,1)} %bitcast.31, bf16[4,1024,256]{2,1,0:T(8,128)(2,1)} %bitcast.12, s32[1,128]{1,0:T(1,128)} %reshape.42.asks, bf16[256,1024]{1,0:T(8,128)(2,1)} %weight.1), custom_call_target="tpu_custom_call" | custom-call | tf_op jit(solution)/shard_map/spread/pallas_call | solution.py:332
  92.9 1.7 dynamic-slice_bitcast_fusion.refs_6_
  94.7 0.0 copy-start
  94.7 98.0 %conditional.1 = (bf16[4,1024,256]{2,1,0:T(8,128)(2,1)}, bf16[128,128,256]{2,1,0:T(8,128)(2,1)}) conditional(s32[]{:T(128)} %bitcast.2, (s32[1024]{0:T(1024)S(1)}, bf16[8,16,128,256]{3,2,1,0:T(8,128)(2,1)}, bf16[4,1024,256]{2,1,0:T(8,128)(2,1)S(1)}) %tuple.87, (bf16[4,1024,256]{2,1,0:T(8,128)(2,1)S(1)}, ...), branch_computations={%region_0.1_spmd, %region_1.2_spmd, %region_2.3_spmd, %region_3.4_... | conditional | bytes 276824128 | solution.py:486
  94.7 1.0 collective-permute-start
  95.7 96.7 %pull.17 = bf16[128,128,256]{2,1,0:T(8,128)(2,1)} custom-call(s32[1024]{0:T(1024)S(1)} %get-tuple-element.105.block_ids, bf16[8,16,128,256]{3,2,1,0:T(8,128)(2,1)} %get-tuple-element.106.hist), custom_call_target="tpu_custom_call" | custom-call | bytes 268435456 | tf_op jit(solution)/shard_map/cond/branch_1_fun/pull/pallas_call | solution.py:436
  192.4 0.0 collective-permute-done
  192.7 0.0 copy-done
  192.7 0.1 copy.11
  192.8 0.7 reshape.37.refs_0_
  193.4 57.8 %layer.1 = bf16[4096,256]{1,0:T(8,128)(2,1)} custom-call(s32[256]{0:T(256)} %reshape.37.refs_0_, s32[64]{0:T(128)} %bitcast.33, bf16[32,128,256]{2,1,0:T(8,128)(2,1)} %bitcast.13, bf16[32,128,256]{2,1,0:T(8,128)(2,1)} %bitcast.8.refs_3_, bf16[128,128,256]{2,1,0:T(8,128)(2,1)} %get-tuple-element.159.refs_4_, bf16[4,4,2,8,128,128]{5,4,3,2,1,0:T(8,128)(2,1)} %bitcast.14, ...), custom_call_target="tpu_custom_call" | custom-call | tf_op jit(solution)/shard_map/layer/pallas_call | solution.py:165
  251.3 3.0 %copy.47 = bf16[4096,256]{1,0:T(8,128)(2,1)} copy(bf16[4096,256]{1,0:T(8,128)(2,1)} %layer.1) | data formatting | bytes 4194304
Async XLA Ops:
  94.7 98.0 %copy-start = (s32[32,8]{0,1:T(8,128)S(1)}, s32[32,8]{0,1:T(8,128)}, u32[]{:S(2)}) copy-start(s32[32,8]{0,1:T(8,128)} %param.28) | copy-start | bytes 3076
  94.7 97.7 %collective-permute-start = (bf16[4,1024,256]{2,1,0:T(8,128)(2,1)S(1)}, bf16[4,1024,256]{2,1,0:T(8,128)(2,1)}, u32[]{:S(2)}, u32[]{:S(2)}) collective-permute-start(bf16[4,1024,256]{2,1,0:T(8,128)(2,1)S(1)} %get-tuple-element.104), channel_id=1, source_target_pairs={{0,4},{4,0},{8,12},{12,8},{16,20},{20,16},{24,28},{28,24},{32,36},... | collective-permute-start | bytes 6291464 | tf_op jit(solution)/shard_map/cond/branch_1_fun/ppermute | solution.py:481

commit v2 on v1

--- a/solution.py
+++ b/solution.py
@@ -16,7 +16,7 @@
 
 
 def layer_kernel(
-    n_mp, src_no, counts, own, partner, pulled, adj, unread, w_rows, my_bias,
+    n_mp, src_idx, own, partner, pulled, adj, unread, w_rows, my_bias,
     out, srcs, tiles, wts, bias, agg_out, agg_in, res_out,
     load_sem, w_sem, bias_send, bias_recv, send_a, recv_a, send_b, recv_b,
 ):
@@ -24,7 +24,6 @@
     per_chunk, kb = adj.shape[2:4]
     nb, n_pulled = own.shape[0], pulled.shape[0]
     n_src = 2 * nb + n_pulled
-    cap = n_pulled // (NY * NZ * NC)
     rows = per_chunk * BLK
 
     def adj_load(q):
@@ -37,7 +36,31 @@
     ]
     for load in loads:
         load.start()
-    for q in range(CHUNKS):
+    adj_load(0).start()
+    srcs[n_src] = jnp.zeros(srcs.shape[1:], srcs.dtype)
+
+    barrier = pltpu.get_barrier_semaphore()
+    for k in range(1, n_mp):
+        pl.semaphore_signal(barrier, inc=1, device_id={"mp": (me + k) % n_mp}, device_id_type=MESH)
+    pl.semaphore_wait(barrier, n_mp - 1)
+
+    def to_bias(k):
+        return pltpu.make_async_remote_copy(
+            src_ref=my_bias,
+            dst_ref=bias.at[k],
+            send_sem=bias_send.at[k - 1],
+            recv_sem=bias_recv.at[k - 1],
+            device_id={"mp": (me + k) % n_mp},
+            device_id_type=MESH,
+        )
+
+    for k in range(1, n_mp):
+        to_bias(k).start()
+    bias[0] = my_bias[...]
+    for load in loads:
+        load.wait()
+    adj_load(0).wait()
+    for q in range(1, CHUNKS):
         adj_load(q).start()
     cols = own.shape[-1]
     w_loads = [
@@ -49,28 +72,6 @@
     ]
     for load in w_loads:
         load.start()
-    srcs[n_src] = jnp.zeros(srcs.shape[1:], srcs.dtype)
-
-    barrier = pltpu.get_barrier_semaphore()
-    for k in range(1, n_mp):
-        pl.semaphore_signal(barrier, inc=1, device_id={"mp": (me + k) % n_mp}, device_id_type=MESH)
-    pl.semaphore_wait(barrier, n_mp - 1)
-
-    def to_bias(k):
-        return pltpu.make_async_remote_copy(
-            src_ref=my_bias,
-            dst_ref=bias.at[k],
-            send_sem=bias_send.at[k - 1],
-            recv_sem=bias_recv.at[k - 1],
-            device_id={"mp": (me + k) % n_mp},
-            device_id_type=MESH,
-        )
-
-    for k in range(1, n_mp):
-        to_bias(k).start()
-    bias[0] = my_bias[...]
-    for load in loads:
-        load.wait()
     for k in range(1, n_mp):
         to_bias(k).wait()
 
@@ -94,21 +95,13 @@
             device_id_type=MESH,
         )
 
-    def place(src):
-        at = jnp.maximum(src - 2 * nb, 0)
-        owner, slot = at // cap, at % cap
-        oy, oz, oc = owner // (NZ * NC), owner // NC % NZ, owner % NC
-        moved = 2 * nb + ((oy * NC + oc) * NZ + oz) * cap + slot
-        moved = jnp.where(slot < counts[owner], moved, n_src)
-        return jnp.where(src < 2 * nb, src, moved)
-
     def aggregate(q, k, dst):
         dev = (me + k) % n_mp
 
         def one(i, carry):
-            first = ((dev * CHUNKS + q) * per_chunk + i) * kb
+            t = (dev * CHUNKS + q) * per_chunk + i
             lhs = jnp.concatenate([tiles[dev, q, i, j] for j in range(kb)], axis=1)
-            rhs = jnp.concatenate([srcs[place(src_no[first + j])] for j in range(kb)], axis=0)
+            rhs = jnp.concatenate([srcs[src_idx[t, j]] for j in range(kb)], axis=0)
             block = jnp.dot(lhs, rhs, preferred_element_type=jnp.float32)
             dst[pl.ds(pl.multiple_of(i * BLK, BLK), BLK), :] = block.astype(dst.dtype)
             return carry
@@ -133,7 +126,8 @@
 
     for q in range(CHUNKS + 1):
         if q < CHUNKS:
-            adj_load(q).wait()
+            if q:
+                adj_load(q).wait()
             for k in (2, 1, 3):
                 aggregate(q, k, agg_out.at[q, k - 1])
                 to_rows(q, k).start()
@@ -149,7 +143,7 @@
             to_columns(q, k).wait()
 
 
-def layer(src_no, counts, own, partner, pulled, adj, unread, wts, bias):
+def layer(src_idx, own, partner, pulled, adj, unread, wts, bias):
     n_mp = wts.shape[0]
     tb, kb = adj.shape[:2]
     adj = adj.reshape(n_mp, CHUNKS, tb // n_mp // CHUNKS, kb, BLK, BLK)
@@ -165,7 +159,7 @@
     return pl.pallas_call(
         kernel,
         out_shape=jax.ShapeDtypeStruct((tb * BLK, width), jnp.bfloat16),
-        in_specs=[pl.BlockSpec(memory_space=pltpu.SMEM)] * 2 + [any_spec] * 6 + [vmem_spec],
+        in_specs=[pl.BlockSpec(memory_space=pltpu.SMEM)] + [any_spec] * 6 + [vmem_spec],
         out_specs=vmem_spec,
         scratch_shapes=[
             pltpu.VMEM((n_src + 1, BLK, width), jnp.bfloat16),
@@ -182,14 +176,14 @@
         ]
         + [pltpu.SemaphoreType.DMA((CHUNKS, n_mp - 1))] * 4,
         compiler_params=pltpu.CompilerParams(
-            collective_id=0, has_side_effects=True, vmem_limit_bytes=60 << 20
+            collective_id=0, has_side_effects=True, vmem_limit_bytes=50 << 20
         ),
         name="layer",
-    )(src_no, counts, own, partner, pulled, adj, unread, wts, bias)
+    )(src_idx, own, partner, pulled, adj, unread, wts, bias)
 
 
 def spread_kernel(
-    hist, feat, asks, weight, hist_z, feat_y, asked, wts,
+    hist, feat, asks, weight, src_no, counts, hist_z, feat_y, asked, wts, src_idx,
     hist_v, feat_v, weight_v, in_sem, own_sem,
     z_send, z_recv, y_send, y_recv, ask_send, ask_recv, w_send, w_recv,
 ):
@@ -277,6 +271,20 @@
             device_id={"mp": (mp + k) % n_mp},
             device_id_type=MESH,
         )
+
+    own_blocks = feat.shape[0] * feat.shape[1] // BLK
+    cap = asks.shape[-1] // counts.shape[0]
+
+    def place(t, carry):
+        for j in range(src_no.shape[1]):
+            src = src_no[t, j]
+            at = jnp.maximum(src - 2 * own_blocks, 0)
+            owner, slot = at // cap, at % cap
+            oy, oz, oc = owner // (NZ * NC), owner // NC % NZ, owner % NC
+            moved = ((oy * NC + oc) * NZ + oz) * cap + slot
+            moved = jnp.where(slot < counts[owner], moved, counts.shape[0] * cap)
+            src_idx[t, j] = jnp.where(src < 2 * own_blocks, src, 2 * own_blocks + moved)
+        return carry
 
     z_ways = [order(NZ, Z_PIECES, up) for up in (True, False)]
     y_ways = [order(NY, Y_PIECES, up) for up in (True, False)]
@@ -302,6 +310,9 @@
             if s > 1:
                 z_hop(up, s - 1, p).wait_recv()
             z_hop(up, s, p).start()
+        some = -(-src_no.shape[0] // (len(z_ways[0]) - Z_AHEAD))
+        first = (i - Z_AHEAD) * some
+        lax.fori_loop(first, min(first + some, src_no.shape[0]), place, 0)
         if i == len(z_ways[0]) * 3 // 4:
             for way in y_ways:
                 for up, s, p in way[Y_PIECES:]:
@@ -322,8 +333,9 @@
         copy.wait()
 
 
-def spread(history, features, asks, weight, n_mp):
+def spread(history, features, asks, weight, src_no, counts, n_mp):
     any_spec = pl.BlockSpec(memory_space=pl.ANY)
+    smem_spec = pl.BlockSpec(memory_space=pltpu.SMEM)
     n_peers = NY * NC - 1
 
     def out(lead, value):
@@ -331,9 +343,10 @@
 
     return pl.pallas_call(
         spread_kernel,
-        out_shape=(out(NZ, history), out(NY, features), out(NY * NC, asks), out(n_mp, weight)),
-        in_specs=[any_spec] * 4,
-        out_specs=(any_spec,) * 4,
+        out_shape=(out(NZ, history), out(NY, features), out(NY * NC, asks), out(n_mp, weight),
+                   jax.ShapeDtypeStruct(src_no.shape, jnp.int32)),
+        in_specs=[any_spec] * 4 + [smem_spec] * 2,
+        out_specs=(any_spec,) * 4 + (smem_spec,),
         scratch_shapes=[
             pltpu.VMEM(history.shape, history.dtype),
             pltpu.VMEM(features.shape, features.dtype),
@@ -353,7 +366,7 @@
             collective_id=2, has_side_effects=True, vmem_limit_bytes=60 << 20
         ),
         name="spread",
-    )(history, features, asks, weight)
+    )(history, features, asks, weight, src_no, counts)
 
 
 def pull_kernel(block_ids, hist, out, *scratch):
@@ -465,11 +478,13 @@
     y_mask = mask >> 4
     zc_mask = mask & (NZ * NC - 1)
 
-    hist_z, feat_y, asked, wts = spread(
+    hist_z, feat_y, asked, wts, src_idx = spread(
         history.reshape(hist_blocks, BLK, width),
         features.reshape(Y_PIECES, row_count // Y_PIECES, width),
         pull_list.reshape(1, -1),
         weight,
+        adj_sources,
+        pull_count[0],
         n_mp,
     )
 
@@ -492,8 +507,7 @@
     )
 
     return layer(
-        adj_sources.reshape(-1),
-        pull_count.reshape(-1),
+        src_idx,
         features.reshape(row_blocks, BLK, width),
         partner_rows.reshape(row_blocks, BLK, width),
         pulled,

time: 254 us -> 254 us (level)
  no operation moved by 1% of the time
where the time goes in v2:
time: 254 us
  Pallas kernels  245 us (96%)
  local copies, waits for them, and re-layouts  5.84 us (2%)
    pallas_call x1, Pallas kernels, pull(): pl.pallas_call(pull_kernel, out_shape=jax.ShapeDtypeStruct((total, BLK, w...  96.8 us
    pallas_call x1, Pallas kernels, spread(): pl.pallas_call(spread_kernel, out_shape=(out(NZ, history), out(NY, featur...  92.6 us
    pallas_call x1, Pallas kernels, layer(): pl.pallas_call(kernel, out_shape=jax.ShapeDtypeStruct((tb * BLK, width),...  55.8 us
  transfers between devices with their start and end apart: 1, of which 0 were waited for; matrix products, arithmetic and copies ran while one was open for 0% of the time, Pallas kernels for 38%

profile of v2, /device:TPU:1, one launch (start us, length us, event | category | flops | bytes accessed | tf_op | source)
XLA Modules:
  0.0 253.8 jit_solution(9807629215574675593)
XLA Ops:
  0.7 1.4 copy.13.src_no
  2.0 0.8 copy.12
  2.8 0.6 reshape.33.asks
  3.4 92.6 %spread.1 = (bf16[8,16,128,256]{3,2,1,0:T(8,128)(2,1)}, bf16[4,4,1024,256]{3,2,1,0:T(8,128)(2,1)}, s32[8,1,128]{2,1,0:T(1,128)S(1)}, bf16[4,256,1024]{2,1,0:T(8,128)(2,1)}, s32[32,8]{1,0:T(8,128)}) custom-call(bf16[16,128,256]{2,1,0:T(8,128)(2,1)} %bitcast.32, bf16[4,1024,256]{2,1,0:T(8,128)(2,1)} %bitcast.13, s32[1,128]{1,0:T(1,128)} %reshape.33.asks, ...), custom_call_target="tpu_custom_call" | custom-call | tf_op jit(solution)/shard_map/spread/pallas_call | solution.py:344
  96.0 1.7 dynamic-slice_bitcast_fusion.refs_5_
  97.8 0.0 copy-start
  97.8 0.0 copy-start.1
  97.8 98.8 %conditional.1 = (bf16[4,1024,256]{2,1,0:T(8,128)(2,1)}, bf16[128,128,256]{2,1,0:T(8,128)(2,1)}) conditional(s32[]{:T(128)} %bitcast.4, (s32[1024]{0:T(1024)S(1)}, bf16[8,16,128,256]{3,2,1,0:T(8,128)(2,1)}, bf16[4,1024,256]{2,1,0:T(8,128)(2,1)S(1)}) %tuple.87, (bf16[4,1024,256]{2,1,0:T(8,128)(2,1)S(1)}, ...), branch_computations={%region_0.1_spmd, %region_1.2_spmd, %region_2.3_spmd, %region_3.4_... | conditional | bytes 276824128 | solution.py:501
  98.0 1.6 collective-permute-start.14
  99.6 96.8 %pull.31 = bf16[128,128,256]{2,1,0:T(8,128)(2,1)} custom-call(s32[1024]{0:T(1024)S(1)} %get-tuple-element.147.block_ids, bf16[8,16,128,256]{3,2,1,0:T(8,128)(2,1)} %get-tuple-element.148.hist), custom_call_target="tpu_custom_call" | custom-call | bytes 268435456 | tf_op jit(solution)/shard_map/cond/branch_15_fun/pull/pallas_call | solution.py:449
  196.4 0.0 collective-permute-done.14
  196.7 0.0 copy-done
  196.7 0.0 copy-done.1
  196.7 55.8 %layer.1 = bf16[4096,256]{1,0:T(8,128)(2,1)S(1)} custom-call(s32[32,8]{1,0:T(8,128)S(1)} %copy-done, bf16[32,128,256]{2,1,0:T(8,128)(2,1)} %bitcast.14, bf16[32,128,256]{2,1,0:T(8,128)(2,1)} %bitcast.8.refs_2_, bf16[128,128,256]{2,1,0:T(8,128)(2,1)} %get-tuple-element.161.refs_3_, bf16[4,4,2,8,128,128]{5,4,3,2,1,0:T(8,128)(2,1)} %bitcast.15, ...), custom_call_target="tpu_custom_call" | custom-call | tf_op jit(solution)/shard_map/layer/pallas_call | solution.py:159
  252.5 1.3 copy.48
Async XLA Ops:
  97.8 98.9 %copy-start = (s32[32,8]{1,0:T(8,128)S(1)}, s32[32,8]{1,0:T(8,128)}, u32[]{:S(2)}) copy-start(s32[32,8]{1,0:T(8,128)} %get-tuple-element.156.refs_0_) | copy-start | bytes 3076
  97.8 98.9 %copy-start.1 = (f32[256]{0:T(256)S(1)}, f32[256]{0:T(256)}, u32[]{:S(2)}) copy-start(f32[256]{0:T(256)} %param.33) | copy-start | bytes 3076
  98.0 98.4 %collective-permute-start.14 = (bf16[4,1024,256]{2,1,0:T(8,128)(2,1)S(1)}, bf16[4,1024,256]{2,1,0:T(8,128)(2,1)}, u32[]{:S(2)}, u32[]{:S(2)}) collective-permute-start(bf16[4,1024,256]{2,1,0:T(8,128)(2,1)S(1)} %get-tuple-element.146), channel_id=1, source_target_pairs={{0,60},{4,56},{8,52},{12,48},{16,44},{20,40},{24,36},{28,32},{32,2... | collective-permute-start | bytes 6291464 | tf_op jit(solution)/shard_map/cond/branch_15_fun/ppermute | solution.py:496

commit v3 on v2

--- a/solution.py
+++ b/solution.py
@@ -16,23 +16,24 @@
 
 
 def layer_kernel(
-    n_mp, src_idx, own, partner, pulled, adj, unread, w_rows, my_bias,
+    n_mp, src_idx, own, partner, near, pulled, adj, unread, w_rows, my_bias,
     out, srcs, tiles, wts, bias, agg_out, agg_in, res_out,
     load_sem, w_sem, bias_send, bias_recv, send_a, recv_a, send_b, recv_b,
 ):
     me = lax.axis_index("mp")
     per_chunk, kb = adj.shape[2:4]
-    nb, n_pulled = own.shape[0], pulled.shape[0]
-    n_src = 2 * nb + n_pulled
+    nb, n_near, n_pulled = own.shape[0], near.shape[0], pulled.shape[0]
+    n_src = 2 * nb + n_near + n_pulled
     rows = per_chunk * BLK
 
     def adj_load(q):
-        return pltpu.make_async_copy(adj.at[:, q], tiles.at[:, q], load_sem.at[3 + q])
+        return pltpu.make_async_copy(adj.at[:, q], tiles.at[:, q], load_sem.at[4 + q])
 
     loads = [
         pltpu.make_async_copy(own, srcs.at[pl.ds(0, nb)], load_sem.at[0]),
         pltpu.make_async_copy(partner, srcs.at[pl.ds(nb, nb)], load_sem.at[1]),
-        pltpu.make_async_copy(pulled, srcs.at[pl.ds(2 * nb, n_pulled)], load_sem.at[2]),
+        pltpu.make_async_copy(near, srcs.at[pl.ds(2 * nb, n_near)], load_sem.at[2]),
+        pltpu.make_async_copy(pulled, srcs.at[pl.ds(2 * nb + n_near, n_pulled)], load_sem.at[3]),
     ]
     for load in loads:
         load.start()
@@ -101,7 +102,7 @@
         def one(i, carry):
             t = (dev * CHUNKS + q) * per_chunk + i
             lhs = jnp.concatenate([tiles[dev, q, i, j] for j in range(kb)], axis=1)
-            rhs = jnp.concatenate([srcs[src_idx[t, j]] for j in range(kb)], axis=0)
+            rhs = jnp.concatenate([srcs[src_idx[j, t]] for j in range(kb)], axis=0)
             block = jnp.dot(lhs, rhs, preferred_element_type=jnp.float32)
             dst[pl.ds(pl.multiple_of(i * BLK, BLK), BLK), :] = block.astype(dst.dtype)
             return carry
@@ -143,12 +144,12 @@
             to_columns(q, k).wait()
 
 
-def layer(src_idx, own, partner, pulled, adj, unread, wts, bias):
+def layer(src_idx, own, partner, near, pulled, adj, unread, wts, bias):
     n_mp = wts.shape[0]
     tb, kb = adj.shape[:2]
     adj = adj.reshape(n_mp, CHUNKS, tb // n_mp // CHUNKS, kb, BLK, BLK)
     width = own.shape[-1]
-    n_src = own.shape[0] + partner.shape[0] + pulled.shape[0]
+    n_src = own.shape[0] + partner.shape[0] + near.shape[0] + pulled.shape[0]
     rows = tb // n_mp // CHUNKS * BLK
     any_spec = pl.BlockSpec(memory_space=pl.ANY)
     vmem_spec = pl.BlockSpec(memory_space=pltpu.VMEM)
@@ -159,7 +160,7 @@
     return pl.pallas_call(
         kernel,
         out_shape=jax.ShapeDtypeStruct((tb * BLK, width), jnp.bfloat16),
-        in_specs=[pl.BlockSpec(memory_space=pltpu.SMEM)] + [any_spec] * 6 + [vmem_spec],
+        in_specs=[pl.BlockSpec(memory_space=pltpu.SMEM)] + [any_spec] * 7 + [vmem_spec],
         out_specs=vmem_spec,
         scratch_shapes=[
             pltpu.VMEM((n_src + 1, BLK, width), jnp.bfloat16),
@@ -169,7 +170,7 @@
             pltpu.VMEM((CHUNKS, n_mp - 1, rows, width), jnp.bfloat16),
             pltpu.VMEM((CHUNKS, n_mp, rows, width), jnp.bfloat16),
             pltpu.VMEM((CHUNKS, n_mp - 1, rows, width), jnp.bfloat16),
-            pltpu.SemaphoreType.DMA((3 + CHUNKS,)),
+            pltpu.SemaphoreType.DMA((4 + CHUNKS,)),
             pltpu.SemaphoreType.DMA((n_mp, n_mp)),
             pltpu.SemaphoreType.DMA((n_mp - 1,)),
             pltpu.SemaphoreType.DMA((n_mp - 1,)),
@@ -179,21 +180,24 @@
             collective_id=0, has_side_effects=True, vmem_limit_bytes=50 << 20
         ),
         name="layer",
-    )(src_idx, own, partner, pulled, adj, unread, wts, bias)
+    )(src_idx, own, partner, near, pulled, adj, unread, wts, bias)
 
 
 def spread_kernel(
-    hist, feat, asks, weight, src_no, counts, hist_z, feat_y, asked, wts, src_idx,
-    hist_v, feat_v, weight_v, in_sem, own_sem,
-    z_send, z_recv, y_send, y_recv, ask_send, ask_recv, w_send, w_recv,
+    hist, feat, asks, weight, src_no, counts, hist_z, feat_y, asked, near, wts, src_idx,
+    hist_v, feat_v, weight_v, asked_s, picked, in_sem, own_sem,
+    z_send, z_recv, y_send, y_recv, ask_send, ask_recv, w_send, w_recv, near_send, near_recv,
 ):
     y, z, core, mp = (lax.axis_index(name) for name in ("y", "z", "core", "mp"))
     n_mp = wts.shape[0]
     z_piece = hist.shape[0] // Z_PIECES
+    n_targets = src_no.shape[1]
+    own_blocks = feat.shape[0] * feat.shape[1] // BLK
+    cap = asks.shape[-1] // counts.shape[0]
     n_peers = NY * NC - 1
 
     def peer(n):
-        at = n + 1
+        at = (n + 1) % (NY * NC)
         return (y + at // NC) % NY, (core + at % NC) % NC
 
     loads = [
@@ -205,8 +209,9 @@
         pltpu.make_async_copy(hist_v, hist_z.at[z], own_sem.at[0]),
         pltpu.make_async_copy(feat_v, feat_y.at[y], own_sem.at[1]),
         pltpu.make_async_copy(weight_v, wts.at[0], own_sem.at[2]),
-        pltpu.make_async_copy(asks, asked.at[y * NC + core], own_sem.at[3]),
+        pltpu.make_async_copy(picked.at[n_peers], near.at[y * NC + core], own_sem.at[4]),
     ]
+    own_ask = pltpu.make_async_copy(asks, asked.at[y * NC + core], own_sem.at[3])
     for load in loads:
         load.start()
 
@@ -272,18 +277,15 @@
             device_id_type=MESH,
         )
 
-    own_blocks = feat.shape[0] * feat.shape[1] // BLK
-    cap = asks.shape[-1] // counts.shape[0]
-
     def place(t, carry):
-        for j in range(src_no.shape[1]):
-            src = src_no[t, j]
+        for j in range(src_no.shape[0]):
+            src = src_no[j, t]
             at = jnp.maximum(src - 2 * own_blocks, 0)
             owner, slot = at // cap, at % cap
             oy, oz, oc = owner // (NZ * NC), owner // NC % NZ, owner % NC
-            moved = ((oy * NC + oc) * NZ + oz) * cap + slot
+            moved = (((z + NZ - oz) % NZ * NY + oy) * NC + oc) * cap + slot
             moved = jnp.where(slot < counts[owner], moved, counts.shape[0] * cap)
-            src_idx[t, j] = jnp.where(src < 2 * own_blocks, src, 2 * own_blocks + moved)
+            src_idx[j, t] = jnp.where(src < 2 * own_blocks, src, 2 * own_blocks + moved)
         return carry
 
     z_ways = [order(NZ, Z_PIECES, up) for up in (True, False)]
@@ -298,8 +300,41 @@
         ask(n).start()
     for k in range(1, n_mp):
         share(k).start()
+    own_ask.start()
     for load in loads:
         load.wait()
+
+    own_ask.wait()
+    for n in range(n_peers):
+        ask(n).wait_recv()
+    index = pltpu.make_async_copy(asked, asked_s, in_sem.at[3])
+    index.start()
+    index.wait()
+
+    def near_give(n):
+        to_y, to_core = peer(n)
+        return pltpu.make_async_remote_copy(
+            src_ref=picked.at[n],
+            dst_ref=near.at[y * NC + core],
+            send_sem=near_send.at[n],
+            recv_sem=near_recv.at[n],
+            device_id={"y": to_y, "core": to_core},
+            device_id_type=MESH,
+        )
+
+    def serve(n, carry):
+        to_y, to_core = peer(n)
+        for slot in range(cap):
+            at = ((y * NZ + z) * NC + core) * cap + slot
+            picked[n, slot] = hist_v[asked_s[to_y * NC + to_core, 0, at]]
+
+        @pl.when(n < n_peers)
+        def _():
+            near_give(n).start()
+
+        return carry
+
+    lax.fori_loop(0, n_peers + 1, serve, 0)
     for copy in own:
         copy.start()
 
@@ -310,9 +345,9 @@
             if s > 1:
                 z_hop(up, s - 1, p).wait_recv()
             z_hop(up, s, p).start()
-        some = -(-src_no.shape[0] // (len(z_ways[0]) - Z_AHEAD))
+        some = -(-n_targets // (len(z_ways[0]) - Z_AHEAD))
         first = (i - Z_AHEAD) * some
-        lax.fori_loop(first, min(first + some, src_no.shape[0]), place, 0)
+        lax.fori_loop(first, min(first + some, n_targets), place, 0)
         if i == len(z_ways[0]) * 3 // 4:
             for way in y_ways:
                 for up, s, p in way[Y_PIECES:]:
@@ -326,7 +361,8 @@
             for hop in way[-ahead:]:
                 make(*hop).wait_send()
     for n in range(n_peers):
-        ask(n).wait()
+        ask(n).wait_send()
+        near_give(n).wait()
     for k in range(1, n_mp):
         share(k).wait()
     for copy in own:
@@ -341,18 +377,23 @@
     def out(lead, value):
         return jax.ShapeDtypeStruct((lead,) + value.shape, value.dtype)
 
+    cap = asks.shape[-1] // counts.shape[0]
+    near = jax.ShapeDtypeStruct((NY * NC, cap) + history.shape[1:], history.dtype)
+
     return pl.pallas_call(
         spread_kernel,
-        out_shape=(out(NZ, history), out(NY, features), out(NY * NC, asks), out(n_mp, weight),
+        out_shape=(out(NZ, history), out(NY, features), out(NY * NC, asks), near, out(n_mp, weight),
                    jax.ShapeDtypeStruct(src_no.shape, jnp.int32)),
         in_specs=[any_spec] * 4 + [smem_spec] * 2,
-        out_specs=(any_spec,) * 4 + (smem_spec,),
+        out_specs=(any_spec,) * 5 + (smem_spec,),
         scratch_shapes=[
             pltpu.VMEM(history.shape, history.dtype),
             pltpu.VMEM(features.shape, features.dtype),
             pltpu.VMEM(weight.shape, weight.dtype),
-            pltpu.SemaphoreType.DMA((3,)),
+            pltpu.SMEM((NY * NC,) + asks.shape, asks.dtype),
+            pltpu.VMEM(near.shape, near.dtype),
             pltpu.SemaphoreType.DMA((4,)),
+            pltpu.SemaphoreType.DMA((5,)),
             pltpu.SemaphoreType.DMA((2, NZ // 2, Z_PIECES)),
             pltpu.SemaphoreType.DMA((2, NZ // 2, Z_PIECES)),
             pltpu.SemaphoreType.DMA((2, NY // 2, Y_PIECES)),
@@ -361,6 +402,8 @@
             pltpu.SemaphoreType.DMA((n_peers,)),
             pltpu.SemaphoreType.DMA((n_mp - 1,)),
             pltpu.SemaphoreType.DMA((n_mp - 1,)),
+            pltpu.SemaphoreType.DMA((n_peers,)),
+            pltpu.SemaphoreType.DMA((n_peers,)),
         ],
         compiler_params=pltpu.CompilerParams(
             collective_id=2, has_side_effects=True, vmem_limit_bytes=60 << 20
@@ -370,9 +413,9 @@
 
 
 def pull_kernel(block_ids, hist, out, *scratch):
-    shards = scratch[:NZ]
-    picked, load_sem, keep_sem, send_sems, recv_sems = scratch[NZ:]
-    y, core = lax.axis_index("y"), lax.axis_index("core")
+    shards = scratch[:NZ - 1]
+    picked, load_sem, keep_sem, send_sems, recv_sems = scratch[NZ - 1:]
+    y, z, core = lax.axis_index("y"), lax.axis_index("z"), lax.axis_index("core")
     cap = picked.shape[2]
     me = y * NC + core
     n_peers = NY * NC - 1
@@ -382,7 +425,10 @@
         at = 3 * (n + 1) % (NC * NY)
         return (y + at // NC) % NY, (core + at % NC) % NC
 
-    loads = [pltpu.make_async_copy(hist.at[r], shards[r], load_sem.at[r]) for r in range(NZ)]
+    loads = [
+        pltpu.make_async_copy(hist.at[(z + NZ - 1 - r) % NZ], shards[r], load_sem.at[r])
+        for r in range(NZ - 1)
+    ]
     for load in loads:
         load.start()
     barrier = pltpu.get_barrier_semaphore()
@@ -394,7 +440,7 @@
     pl.semaphore_wait(barrier, n_peers)
 
     def rows(r):
-        return out.at[pl.ds((me * NZ + r) * cap, cap)]
+        return out.at[pl.ds((r * (n_peers + 1) + me) * cap, cap)]
 
     def give(r, n):
         to_y, to_core = peer(n)
@@ -410,12 +456,12 @@
     def keep(r):
         return pltpu.make_async_copy(picked.at[r, n_peers], rows(r), keep_sem.at[r])
 
-    for r in range(NZ):
+    for r in range(NZ - 1):
         loads[r].wait()
 
         def one(n, carry):
             to_y, to_core = peer(n)
-            first = (to_y * NC + to_core) * per_ask + ((y * NZ + r) * NC + core) * cap
+            first = (to_y * NC + to_core) * per_ask + ((y * NZ + (z + NZ - 1 - r) % NZ) * NC + core) * cap
             for slot in range(cap):
                 picked[r, n, slot] = shards[r][block_ids[first + slot]]
 
@@ -437,7 +483,7 @@
         keep(r).wait()
         return carry
 
-    lax.fori_loop(0, NZ, finish, 0)
+    lax.fori_loop(0, NZ - 1, finish, 0)
 
 
 def pull(block_ids, hist):
@@ -448,16 +494,16 @@
     any_spec = pl.BlockSpec(memory_space=pl.ANY)
     return pl.pallas_call(
         pull_kernel,
-        out_shape=jax.ShapeDtypeStruct((total, BLK, width), jnp.bfloat16),
+        out_shape=jax.ShapeDtypeStruct((total // NZ * (NZ - 1), BLK, width), jnp.bfloat16),
         in_specs=[pl.BlockSpec(memory_space=pltpu.SMEM), any_spec],
         out_specs=any_spec,
-        scratch_shapes=[pltpu.VMEM(hist.shape[1:], jnp.bfloat16)] * NZ
+        scratch_shapes=[pltpu.VMEM(hist.shape[1:], jnp.bfloat16)] * (NZ - 1)
         + [
-            pltpu.VMEM((NZ, n_peers, cap, BLK, width), jnp.bfloat16),
-            pltpu.SemaphoreType.DMA((NZ,)),
-            pltpu.SemaphoreType.DMA((NZ,)),
-            pltpu.SemaphoreType.DMA((NZ, n_peers - 1)),
-            pltpu.SemaphoreType.DMA((NZ, n_peers - 1)),
+            pltpu.VMEM((NZ - 1, n_peers, cap, BLK, width), jnp.bfloat16),
+            pltpu.SemaphoreType.DMA((NZ - 1,)),
+            pltpu.SemaphoreType.DMA((NZ - 1,)),
+            pltpu.SemaphoreType.DMA((NZ - 1, n_peers - 1)),
+            pltpu.SemaphoreType.DMA((NZ - 1, n_peers - 1)),
         ],
         compiler_params=pltpu.CompilerParams(
             collective_id=1, has_side_effects=True, vmem_limit_bytes=60 << 20
@@ -478,12 +524,12 @@
     y_mask = mask >> 4
     zc_mask = mask & (NZ * NC - 1)
 
-    hist_z, feat_y, asked, wts, src_idx = spread(
+    hist_z, feat_y, asked, near, wts, src_idx = spread(
         history.reshape(hist_blocks, BLK, width),
         features.reshape(Y_PIECES, row_count // Y_PIECES, width),
         pull_list.reshape(1, -1),
         weight,
-        adj_sources,
+        adj_sources.T,
         pull_count[0],
         n_mp,
     )
@@ -510,6 +556,7 @@
         src_idx,
         features.reshape(row_blocks, BLK, width),
         partner_rows.reshape(row_blocks, BLK, width),
+        near.reshape(-1, BLK, width),
         pulled,
         adj_values,
         half_way,

time: 254 us -> 287 us (1.13)
  Pallas kernels: 245 us -> 269 us
  waiting for transfers between devices: 0.01 us -> 9.01 us
    pallas_call x1, Pallas kernels: 92.6 us -> 130 us  [spread(): pl.pallas_call(spread_kernel, out_shape=(out(NZ, history), out(NY, featur...]
    pallas_call x1, Pallas kernels: 96.8 us -> 85.2 us  [pull(): pl.pallas_call(pull_kernel, out_shape=jax.ShapeDtypeStruct((total // NZ *...]
    ppermute x1, waiting for transfers between devices: 0.01 us -> 9.01 us  [branch(): lax.ppermute(rows, ('z', 'core'), [(s, s ^ m) for s in range(NZ * NC)])]
  transfers between devices with their start and end apart: 1 -> 1, of which waited for: 0 -> 1; matrix products, arithmetic and copies ran while one was open for 0% -> 0% of each run, Pallas kernels for 38% -> 30%
where the time goes in v3:
time: 287 us; the launch traced here: 286 us
  Pallas kernels  269 us (94%)
  waiting for transfers between devices  9.01 us (3%)
  local copies, waits for them, and re-layouts  4.49 us (2%)
  starting transfers between devices  3.07 us (1%)
    pallas_call x1, Pallas kernels, spread(): pl.pallas_call(spread_kernel, out_shape=(out(NZ, history), out(NY, featur...  130 us
    pallas_call x1, Pallas kernels, pull(): pl.pallas_call(pull_kernel, out_shape=jax.ShapeDtypeStruct((total // NZ *...  85.2 us
    pallas_call x1, Pallas kernels, layer(): pl.pallas_call(kernel, out_shape=jax.ShapeDtypeStruct((tb * BLK, width),...  53.1 us
    ppermute x1, waiting for transfers between devices, branch(): lax.ppermute(rows, ('z', 'core'), [(s, s ^ m) for s in range(NZ * NC)])  9.01 us
  transfers between devices with their start and end apart: 1, of which 1 were waited for; matrix products, arithmetic and copies ran while one was open for 0% of the time, Pallas kernels for 30%

profile of v3, /device:TPU:1, one launch (start us, length us, event | category | flops | bytes accessed | tf_op | source)
XLA Modules:
  0.0 286.3 jit_solution(17719543440992654297)
XLA Ops:
  0.7 0.8 copy.11
  1.4 0.7 reshape.36.asks
  2.1 130.5 %spread.1 = (bf16[8,16,128,256]{3,2,1,0:T(8,128)(2,1)}, bf16[4,4,1024,256]{3,2,1,0:T(8,128)(2,1)}, s32[8,1,128]{2,1,0:T(1,128)S(1)}, bf16[8,2,128,256]{3,2,1,0:T...) custom-call(bf16[16,128,256]{2,1,0:T(8,128)(2,1)} %bitcast.35, bf16[4,1024,256]{2,1,0:T(8,128)(2,1)} %bitcast.17, ...), custom_call_target="tpu_custom_call" | custom-call | tf_op jit(solution)/shard_map/spread/pallas_call | solution.py:383
  132.5 1.7 dynamic-slice_bitcast_fusion.refs_6_
  134.3 0.0 copy-start
  134.3 0.0 copy-start.1
  134.3 0.0 copy-start.2
  134.3 97.6 %conditional.1 = (bf16[4,1024,256]{2,1,0:T(8,128)(2,1)}, bf16[112,128,256]{2,1,0:T(8,128)(2,1)}) conditional(s32[]{:T(128)} %bitcast.5, (s32[1024]{0:T(1024)S(1)}, bf16[8,16,128,256]{3,2,1,0:T(8,128)(2,1)}, bf16[4,1024,256]{2,1,0:T(8,128)(2,1)S(1)}) %tuple.87, (bf16[4,1024,256]{2,1,0:T(8,128)(2,1)S(1)}, ...), branch_computations={%region_0.1_spmd, %region_1.2_spmd, %region_2.3_spmd, %region_3.4_... | conditional | bytes 276824128 | solution.py:547
  134.5 3.1 %collective-permute-start.8 = (bf16[4,1024,256]{2,1,0:T(8,128)(2,1)S(1)}, bf16[4,1024,256]{2,1,0:T(8,128)(2,1)}, u32[]{:S(2)}, u32[]{:S(2)}) collective-permute-start(bf16[4,1024,256]{2,1,0:T(8,128)(2,1)S(1)} %get-tuple-element.128), channel_id=1, source_target_pairs={{0,36},{4,32},{8,44},{12,40},{16,52},{20,48},{24,60},{28,56},{32,4... | collective-permute-start | bytes 6291464 | tf_op jit(solution)/shard_map/cond/branch_9_fun/ppermute | solution.py:542
  137.6 85.2 %pull.25 = bf16[112,128,256]{2,1,0:T(8,128)(2,1)} custom-call(s32[1024]{0:T(1024)S(1)} %get-tuple-element.129.block_ids, bf16[8,16,128,256]{3,2,1,0:T(8,128)(2,1)} %get-tuple-element.130.hist), custom_call_target="tpu_custom_call" | custom-call | bytes 268435456 | tf_op jit(solution)/shard_map/cond/branch_9_fun/pull/pallas_call | solution.py:495
  222.9 9.0 %collective-permute-done.8 = bf16[4,1024,256]{2,1,0:T(8,128)(2,1)} collective-permute-done((bf16[4,1024,256]{2,1,0:T(8,128)(2,1)S(1)}, bf16[4,1024,256]{2,1,0:T(8,128)(2,1)}, u32[]{:S(2)}, u32[]{:S(2)}) %collective-permute-start.8) | collective-permute-done | bytes 2097184 | tf_op jit(solution)/shard_map/cond/branch_9_fun/ppermute | solution.py:542
  231.9 0.0 copy-done
  231.9 0.0 copy-done.1
  231.9 0.0 copy-done.2
  231.9 53.1 %layer.1 = bf16[4096,256]{1,0:T(8,128)(2,1)S(1)} custom-call(s32[8,32]{1,0:T(8,128)S(1)} %copy-done.1, bf16[32,128,256]{2,1,0:T(8,128)(2,1)} %bitcast.18, bf16[32,128,256]{2,1,0:T(8,128)(2,1)} %bitcast.9.refs_2_, bf16[16,128,256]{2,1,0:T(8,128)(2,1)S(1)} %bitcast.14, bf16[112,128,256]{2,1,0:T(8,128)(2,1)} %get-tuple-element.163.refs_4_, ...), custom_call_target="tpu_custom_call" | custom-call | tf_op jit(solution)/shard_map/layer/pallas_call | solution.py:160
  284.9 1.3 copy.46
Async XLA Ops:
  134.3 97.6 %copy-start = (bf16[8,2,128,256]{3,2,1,0:T(8,128)(2,1)S(1)}, bf16[8,2,128,256]{3,2,1,0:T(8,128)(2,1)}, u32[]{:S(2)}) copy-start(bf16[8,2,128,256]{3,2,1,0:T(8,128)(2,1)} %get-tuple-element.162) | copy-start | bytes 3145732
  134.3 97.6 %copy-start.1 = (s32[8,32]{1,0:T(8,128)S(1)}, s32[8,32]{1,0:T(8,128)}, u32[]{:S(2)}) copy-start(s32[8,32]{1,0:T(8,128)} %get-tuple-element.157.refs_0_) | copy-start | bytes 3076
  134.3 97.6 %copy-start.2 = (f32[256]{0:T(256)S(1)}, f32[256]{0:T(256)}, u32[]{:S(2)}) copy-start(f32[256]{0:T(256)} %param.33) | copy-start | bytes 3076
  134.5 97.3 %collective-permute-start.8 = (bf16[4,1024,256]{2,1,0:T(8,128)(2,1)S(1)}, bf16[4,1024,256]{2,1,0:T(8,128)(2,1)}, u32[]{:S(2)}, u32[]{:S(2)}) collective-permute-start(bf16[4,1024,256]{2,1,0:T(8,128)(2,1)S(1)} %get-tuple-element.128), channel_id=1, source_target_pairs={{0,36},{4,32},{8,44},{12,40},{16,52},{20,48},{24,60},{28,56},{32,4... | collective-permute-start | bytes 6291464 | tf_op jit(solution)/shard_map/cond/branch_9_fun/ppermute | solution.py:542

commit v4 on v3

--- a/solution.py
+++ b/solution.py
@@ -290,23 +290,23 @@
 
     z_ways = [order(NZ, Z_PIECES, up) for up in (True, False)]
     y_ways = [order(NY, Y_PIECES, up) for up in (True, False)]
+    for n in range(n_peers):
+        ask(n).start()
+    own_ask.start()
     for way in z_ways:
         for hop in way[:Z_AHEAD]:
             z_hop(*hop).start()
+    for load in loads:
+        load.wait()
+
+    own_ask.wait()
+    for n in range(n_peers):
+        ask(n).wait_recv()
     for way in y_ways:
         for hop in way[:Y_PIECES]:
             y_hop(*hop).start()
-    for n in range(n_peers):
-        ask(n).start()
     for k in range(1, n_mp):
         share(k).start()
-    own_ask.start()
-    for load in loads:
-        load.wait()
-
-    own_ask.wait()
-    for n in range(n_peers):
-        ask(n).wait_recv()
     index = pltpu.make_async_copy(asked, asked_s, in_sem.at[3])
     index.start()
     index.wait()

time: 287 us -> 249 us (0.87)
  Pallas kernels: 269 us -> 237 us
  waiting for transfers between devices: 9.01 us -> 6.09 us
    pallas_call x1, Pallas kernels: 130 us -> 94.5 us  [spread(): pl.pallas_call(spread_kernel, out_shape=(out(NZ, history), out(NY, featur...]
    ppermute x1, waiting for transfers between devices: 9.01 us -> 6.09 us  [branch(): lax.ppermute(rows, ('z', 'core'), [(s, s ^ m) for s in range(NZ * NC)])]
  transfers between devices with their start and end apart: 1 -> 1, of which waited for: 1 -> 1; matrix products, arithmetic and copies ran while one was open for 0% -> 0% of each run, Pallas kernels for 30% -> 35%
where the time goes in v4:
time: 249 us; the launch traced here: 248 us
  Pallas kernels  237 us (95%)
  waiting for transfers between devices  6.09 us (2%)
  local copies, waits for them, and re-layouts  4.49 us (2%)
    pallas_call x1, Pallas kernels, spread(): pl.pallas_call(spread_kernel, out_shape=(out(NZ, history), out(NY, featur...  94.5 us
    pallas_call x1, Pallas kernels, pull(): pl.pallas_call(pull_kernel, out_shape=jax.ShapeDtypeStruct((total // NZ *...  86.5 us
    pallas_call x1, Pallas kernels, layer(): pl.pallas_call(kernel, out_shape=jax.ShapeDtypeStruct((tb * BLK, width),...  55.7 us
    ppermute x1, waiting for transfers between devices, branch(): lax.ppermute(rows, ('z', 'core'), [(s, s ^ m) for s in range(NZ * NC)])  6.09 us
  transfers between devices with their start and end apart: 1, of which 1 were waited for; matrix products, arithmetic and copies ran while one was open for 0% of the time, Pallas kernels for 35%

profile of v4, /device:TPU:1, one launch (start us, length us, event | category | flops | bytes accessed | tf_op | source)
XLA Modules:
  0.0 248.3 jit_solution(4471534768917524598)
XLA Ops:
  0.7 0.8 copy.11
  1.4 0.7 reshape.36.asks
  2.1 94.5 %spread.1 = (bf16[8,16,128,256]{3,2,1,0:T(8,128)(2,1)}, bf16[4,4,1024,256]{3,2,1,0:T(8,128)(2,1)}, s32[8,1,128]{2,1,0:T(1,128)S(1)}, bf16[8,2,128,256]{3,2,1,0:T...) custom-call(bf16[16,128,256]{2,1,0:T(8,128)(2,1)} %bitcast.35, bf16[4,1024,256]{2,1,0:T(8,128)(2,1)} %bitcast.17, ...), custom_call_target="tpu_custom_call" | custom-call | tf_op jit(solution)/shard_map/spread/pallas_call | solution.py:383
  96.6 1.7 dynamic-slice_bitcast_fusion.refs_6_
  98.4 0.0 copy-start
  98.4 0.0 copy-start.1
  98.4 0.0 copy-start.2
  98.4 92.9 %conditional.1 = (bf16[4,1024,256]{2,1,0:T(8,128)(2,1)}, bf16[112,128,256]{2,1,0:T(8,128)(2,1)}) conditional(s32[]{:T(128)} %bitcast.5, (s32[1024]{0:T(1024)S(1)}, bf16[8,16,128,256]{3,2,1,0:T(8,128)(2,1)}, bf16[4,1024,256]{2,1,0:T(8,128)(2,1)S(1)}) %tuple.87, (bf16[4,1024,256]{2,1,0:T(8,128)(2,1)S(1)}, ...), branch_computations={%region_0.1_spmd, %region_1.2_spmd, %region_2.3_spmd, %region_3.4_... | conditional | bytes 276824128 | solution.py:547
  98.4 0.3 collective-permute-start.3
  98.7 86.5 %pull.20 = bf16[112,128,256]{2,1,0:T(8,128)(2,1)} custom-call(s32[1024]{0:T(1024)S(1)} %get-tuple-element.114.block_ids, bf16[8,16,128,256]{3,2,1,0:T(8,128)(2,1)} %get-tuple-element.115.hist), custom_call_target="tpu_custom_call" | custom-call | bytes 268435456 | tf_op jit(solution)/shard_map/cond/branch_4_fun/pull/pallas_call | solution.py:495
  185.2 6.1 %collective-permute-done.3 = bf16[4,1024,256]{2,1,0:T(8,128)(2,1)} collective-permute-done((bf16[4,1024,256]{2,1,0:T(8,128)(2,1)S(1)}, bf16[4,1024,256]{2,1,0:T(8,128)(2,1)}, u32[]{:S(2)}, u32[]{:S(2)}) %collective-permute-start.3) | collective-permute-done | bytes 2097184 | tf_op jit(solution)/shard_map/cond/branch_4_fun/ppermute | solution.py:542
  191.3 0.0 copy-done
  191.3 0.0 copy-done.1
  191.3 0.0 copy-done.2
  191.3 55.7 %layer.1 = bf16[4096,256]{1,0:T(8,128)(2,1)S(1)} custom-call(s32[8,32]{1,0:T(8,128)S(1)} %copy-done.1, bf16[32,128,256]{2,1,0:T(8,128)(2,1)} %bitcast.18, bf16[32,128,256]{2,1,0:T(8,128)(2,1)} %bitcast.9.refs_2_, bf16[16,128,256]{2,1,0:T(8,128)(2,1)S(1)} %bitcast.14, bf16[112,128,256]{2,1,0:T(8,128)(2,1)} %get-tuple-element.163.refs_4_, ...), custom_call_target="tpu_custom_call" | custom-call | tf_op jit(solution)/shard_map/layer/pallas_call | solution.py:160
  247.0 1.3 copy.46
Async XLA Ops:
  98.4 92.9 %copy-start = (bf16[8,2,128,256]{3,2,1,0:T(8,128)(2,1)S(1)}, bf16[8,2,128,256]{3,2,1,0:T(8,128)(2,1)}, u32[]{:S(2)}) copy-start(bf16[8,2,128,256]{3,2,1,0:T(8,128)(2,1)} %get-tuple-element.162) | copy-start | bytes 3145732
  98.4 92.9 %copy-start.1 = (s32[8,32]{1,0:T(8,128)S(1)}, s32[8,32]{1,0:T(8,128)}, u32[]{:S(2)}) copy-start(s32[8,32]{1,0:T(8,128)} %get-tuple-element.157.refs_0_) | copy-start | bytes 3076
  98.4 92.9 %copy-start.2 = (f32[256]{0:T(256)S(1)}, f32[256]{0:T(256)}, u32[]{:S(2)}) copy-start(f32[256]{0:T(256)} %param.33) | copy-start | bytes 3076
  98.4 92.9 %collective-permute-start.3 = (bf16[4,1024,256]{2,1,0:T(8,128)(2,1)S(1)}, bf16[4,1024,256]{2,1,0:T(8,128)(2,1)}, u32[]{:S(2)}, u32[]{:S(2)}) collective-permute-start(bf16[4,1024,256]{2,1,0:T(8,128)(2,1)S(1)} %get-tuple-element.113), channel_id=1, source_target_pairs={{0,16},{4,20},{8,24},{12,28},{16,0},{20,4},{24,8},{28,12},{32,48},... | collective-permute-start | bytes 6291464 | tf_op jit(solution)/shard_map/cond/branch_4_fun/ppermute | solution.py:542

commit v5 on v4

--- a/solution.py
+++ b/solution.py
@@ -8,6 +8,7 @@
 NY, NZ, NC = 4, 8, 2
 BLK = 128
 CHUNKS = 4
+LOADS = 4
 Z_PIECES = 4
 Z_AHEAD = 2
 Y_PIECES = 4
@@ -27,14 +28,22 @@
     rows = per_chunk * BLK
 
     def adj_load(q):
-        return pltpu.make_async_copy(adj.at[:, q], tiles.at[:, q], load_sem.at[4 + q])
+        return pltpu.make_async_copy(adj.at[:, q], tiles.at[:, q], load_sem.at[3 + LOADS + q])
 
     loads = [
         pltpu.make_async_copy(own, srcs.at[pl.ds(0, nb)], load_sem.at[0]),
         pltpu.make_async_copy(partner, srcs.at[pl.ds(nb, nb)], load_sem.at[1]),
         pltpu.make_async_copy(near, srcs.at[pl.ds(2 * nb, n_near)], load_sem.at[2]),
-        pltpu.make_async_copy(pulled, srcs.at[pl.ds(2 * nb + n_near, n_pulled)], load_sem.at[3]),
     ]
+    part = n_pulled // LOADS
+    for i in range(LOADS):
+        loads.append(
+            pltpu.make_async_copy(
+                pulled.at[pl.ds(i * part, part)],
+                srcs.at[pl.ds(2 * nb + n_near + i * part, part)],
+                load_sem.at[3 + i],
+            )
+        )
     for load in loads:
         load.start()
     adj_load(0).start()
@@ -170,7 +179,7 @@
             pltpu.VMEM((CHUNKS, n_mp - 1, rows, width), jnp.bfloat16),
             pltpu.VMEM((CHUNKS, n_mp, rows, width), jnp.bfloat16),
             pltpu.VMEM((CHUNKS, n_mp - 1, rows, width), jnp.bfloat16),
-            pltpu.SemaphoreType.DMA((4 + CHUNKS,)),
+            pltpu.SemaphoreType.DMA((3 + LOADS + CHUNKS,)),
             pltpu.SemaphoreType.DMA((n_mp, n_mp)),
             pltpu.SemaphoreType.DMA((n_mp - 1,)),
             pltpu.SemaphoreType.DMA((n_mp - 1,)),
@@ -334,8 +343,7 @@
 
         return carry
 
-    lax.fori_loop(0, n_peers + 1, serve, 0)
-    for copy in own:
+    for copy in own[:-1]:
         copy.start()
 
     for i in range(Z_AHEAD, len(z_ways[0])):
@@ -353,6 +361,8 @@
                 for up, s, p in way[Y_PIECES:]:
                     y_hop(up, s - 1, p).wait_recv()
                     y_hop(up, s, p).start()
+            lax.fori_loop(0, n_peers + 1, serve, 0)
+            own[-1].start()
     for make, ways, ahead in ((z_hop, z_ways, Z_AHEAD), (y_hop, y_ways, len(y_ways[0]))):
         for way in ways:
             for up, s, p in way:

time: 249 us -> 244 us (0.980)
  waiting for transfers between devices: 6.09 us -> 0.01 us
    ppermute x1, waiting for transfers between devices: 6.09 us -> 0.01 us  [branch(): lax.ppermute(rows, ('z', 'core'), [(s, s ^ m) for s in range(NZ * NC)])]
    pallas_call x1, Pallas kernels: 94.5 us -> 97.3 us  [spread(): pl.pallas_call(spread_kernel, out_shape=(out(NZ, history), out(NY, featur...]
  transfers between devices with their start and end apart: 1 -> 1, of which waited for: 1 -> 0; matrix products, arithmetic and copies ran while one was open for 0% -> 0% of each run, Pallas kernels for 35% -> 35%
where the time goes in v5:
time: 244 us
  Pallas kernels  238 us (98%)
  local copies, waits for them, and re-layouts  4.49 us (2%)
    pallas_call x1, Pallas kernels, spread(): pl.pallas_call(spread_kernel, out_shape=(out(NZ, history), out(NY, featur...  97.3 us
    pallas_call x1, Pallas kernels, pull(): pl.pallas_call(pull_kernel, out_shape=jax.ShapeDtypeStruct((total // NZ *...  85.4 us
    pallas_call x1, Pallas kernels, layer(): pl.pallas_call(kernel, out_shape=jax.ShapeDtypeStruct((tb * BLK, width),...  55.5 us
  transfers between devices with their start and end apart: 1, of which 0 were waited for; matrix products, arithmetic and copies ran while one was open for 0% of the time, Pallas kernels for 35%

profile of v5, /device:TPU:1, one launch (start us, length us, event | category | flops | bytes accessed | tf_op | source)
XLA Modules:
  0.0 244.0 jit_solution(10961055021939392731)
XLA Ops:
  0.7 0.8 copy.11
  1.4 0.7 reshape.36.asks
  2.1 97.3 %spread.1 = (bf16[8,16,128,256]{3,2,1,0:T(8,128)(2,1)}, bf16[4,4,1024,256]{3,2,1,0:T(8,128)(2,1)}, s32[8,1,128]{2,1,0:T(1,128)S(1)}, bf16[8,2,128,256]{3,2,1,0:T...) custom-call(bf16[16,128,256]{2,1,0:T(8,128)(2,1)} %bitcast.35, bf16[4,1024,256]{2,1,0:T(8,128)(2,1)} %bitcast.17, ...), custom_call_target="tpu_custom_call" | custom-call | tf_op jit(solution)/shard_map/spread/pallas_call | solution.py:393
  99.4 1.7 dynamic-slice_bitcast_fusion.refs_6_
  101.1 0.0 copy-start
  101.1 0.0 copy-start.1
  101.1 0.0 copy-start.2
  101.1 85.9 %conditional.1 = (bf16[4,1024,256]{2,1,0:T(8,128)(2,1)}, bf16[112,128,256]{2,1,0:T(8,128)(2,1)}) conditional(s32[]{:T(128)} %bitcast.5, (s32[1024]{0:T(1024)S(1)}, bf16[8,16,128,256]{3,2,1,0:T(8,128)(2,1)}, bf16[4,1024,256]{2,1,0:T(8,128)(2,1)S(1)}) %tuple.87, (bf16[4,1024,256]{2,1,0:T(8,128)(2,1)S(1)}, ...), branch_computations={%region_0.1_spmd, %region_1.2_spmd, %region_2.3_spmd, %region_3.4_... | conditional | bytes 276824128 | solution.py:557
  101.2 0.1 collective-permute-start
  101.3 85.4 %pull.17 = bf16[112,128,256]{2,1,0:T(8,128)(2,1)} custom-call(s32[1024]{0:T(1024)S(1)} %get-tuple-element.105.block_ids, bf16[8,16,128,256]{3,2,1,0:T(8,128)(2,1)} %get-tuple-element.106.hist), custom_call_target="tpu_custom_call" | custom-call | bytes 268435456 | tf_op jit(solution)/shard_map/cond/branch_1_fun/pull/pallas_call | solution.py:505
  186.6 0.0 collective-permute-done
  187.1 0.0 copy-done
  187.1 0.0 copy-done.1
  187.1 0.0 copy-done.2
  187.1 55.5 %layer.1 = bf16[4096,256]{1,0:T(8,128)(2,1)S(1)} custom-call(s32[8,32]{1,0:T(8,128)S(1)} %copy-done.1, bf16[32,128,256]{2,1,0:T(8,128)(2,1)} %bitcast.18, bf16[32,128,256]{2,1,0:T(8,128)(2,1)} %bitcast.9.refs_2_, bf16[16,128,256]{2,1,0:T(8,128)(2,1)S(1)} %bitcast.14, bf16[112,128,256]{2,1,0:T(8,128)(2,1)} %get-tuple-element.163.refs_4_, ...), custom_call_target="tpu_custom_call" | custom-call | tf_op jit(solution)/shard_map/layer/pallas_call | solution.py:169
  242.7 1.3 copy.46
Async XLA Ops:
  101.1 86.0 %copy-start = (bf16[8,2,128,256]{3,2,1,0:T(8,128)(2,1)S(1)}, bf16[8,2,128,256]{3,2,1,0:T(8,128)(2,1)}, u32[]{:S(2)}) copy-start(bf16[8,2,128,256]{3,2,1,0:T(8,128)(2,1)} %get-tuple-element.162) | copy-start | bytes 3145732
  101.1 86.0 %copy-start.1 = (s32[8,32]{1,0:T(8,128)S(1)}, s32[8,32]{1,0:T(8,128)}, u32[]{:S(2)}) copy-start(s32[8,32]{1,0:T(8,128)} %get-tuple-element.157.refs_0_) | copy-start | bytes 3076
  101.1 86.0 %copy-start.2 = (f32[256]{0:T(256)S(1)}, f32[256]{0:T(256)}, u32[]{:S(2)}) copy-start(f32[256]{0:T(256)} %param.33) | copy-start | bytes 3076
  101.2 85.5 %collective-permute-start = (bf16[4,1024,256]{2,1,0:T(8,128)(2,1)S(1)}, bf16[4,1024,256]{2,1,0:T(8,128)(2,1)}, u32[]{:S(2)}, u32[]{:S(2)}) collective-permute-start(bf16[4,1024,256]{2,1,0:T(8,128)(2,1)S(1)} %get-tuple-element.104), channel_id=1, source_target_pairs={{0,4},{4,0},{8,12},{12,8},{16,20},{20,16},{24,28},{28,24},{32,36},... | collective-permute-start | bytes 6291464 | tf_op jit(solution)/shard_map/cond/branch_1_fun/ppermute | solution.py:552

commit v6 on v4

--- a/solution.py
+++ b/solution.py
@@ -107,7 +107,7 @@
             dst[pl.ds(pl.multiple_of(i * BLK, BLK), BLK), :] = block.astype(dst.dtype)
             return carry
 
-        lax.fori_loop(0, per_chunk, one, 0)
+        lax.fori_loop(0, per_chunk, one, 0, unroll=True)
 
     def multiply(q):
         for k in range(1, n_mp):

time: 249 us -> 250 us (level)
  starting transfers between devices: 0.28 us -> 4.4 us
  Pallas kernels: 237 us -> 234 us
    ppermute x1, starting transfers between devices: 0.28 us -> 4.4 us  [branch(): lax.ppermute(rows, ('z', 'core'), [(s, s ^ m) for s in range(NZ * NC)])]
  transfers between devices with their start and end apart: 1 -> 1, of which waited for: 1 -> 1; matrix products, arithmetic and copies ran while one was open for 0% -> 0% of each run, Pallas kernels for 35% -> 34%
where the time goes in v6:
time: 250 us; the launch traced here: 249 us
  Pallas kernels  234 us (94%)
  waiting for transfers between devices  4.81 us (2%)
  local copies, waits for them, and re-layouts  4.49 us (2%)
  starting transfers between devices  4.4 us (2%)
    pallas_call x1, Pallas kernels, spread(): pl.pallas_call(spread_kernel, out_shape=(out(NZ, history), out(NY, featur...  94.5 us
    pallas_call x1, Pallas kernels, pull(): pl.pallas_call(pull_kernel, out_shape=jax.ShapeDtypeStruct((total // NZ *...  85.1 us
    pallas_call x1, Pallas kernels, layer(): pl.pallas_call(kernel, out_shape=jax.ShapeDtypeStruct((tb * BLK, width),...  54.7 us
  transfers between devices with their start and end apart: 1, of which 1 were waited for; matrix products, arithmetic and copies ran while one was open for 0% of the time, Pallas kernels for 34%

profile of v6, /device:TPU:1, one launch (start us, length us, event | category | flops | bytes accessed | tf_op | source)
XLA Modules:
  0.0 249.0 jit_solution(16895589695743531344)
XLA Ops:
  0.7 0.8 copy.11
  1.4 0.7 reshape.36.asks
  2.1 94.5 %spread.1 = (bf16[8,16,128,256]{3,2,1,0:T(8,128)(2,1)}, bf16[4,4,1024,256]{3,2,1,0:T(8,128)(2,1)}, s32[8,1,128]{2,1,0:T(1,128)S(1)}, bf16[8,2,128,256]{3,2,1,0:T...) custom-call(bf16[16,128,256]{2,1,0:T(8,128)(2,1)} %bitcast.35, bf16[4,1024,256]{2,1,0:T(8,128)(2,1)} %bitcast.17, ...), custom_call_target="tpu_custom_call" | custom-call | tf_op jit(solution)/shard_map/spread/pallas_call | solution.py:383
  96.6 1.7 dynamic-slice_bitcast_fusion.refs_6_
  98.4 0.0 copy-start
  98.4 0.0 copy-start.1
  98.4 0.0 copy-start.2
  98.4 94.5 %conditional.1 = (bf16[4,1024,256]{2,1,0:T(8,128)(2,1)}, bf16[112,128,256]{2,1,0:T(8,128)(2,1)}) conditional(s32[]{:T(128)} %bitcast.5, (s32[1024]{0:T(1024)S(1)}, bf16[8,16,128,256]{3,2,1,0:T(8,128)(2,1)}, bf16[4,1024,256]{2,1,0:T(8,128)(2,1)S(1)}) %tuple.87, (bf16[4,1024,256]{2,1,0:T(8,128)(2,1)S(1)}, ...), branch_computations={%region_0.1_spmd, %region_1.2_spmd, %region_2.3_spmd, %region_3.4_... | conditional | bytes 276824128 | solution.py:547
  98.6 4.4 %collective-permute-start.12 = (bf16[4,1024,256]{2,1,0:T(8,128)(2,1)S(1)}, bf16[4,1024,256]{2,1,0:T(8,128)(2,1)}, u32[]{:S(2)}, u32[]{:S(2)}) collective-permute-start(bf16[4,1024,256]{2,1,0:T(8,128)(2,1)S(1)} %get-tuple-element.140), channel_id=1, source_target_pairs={{0,52},{4,48},{8,60},{12,56},{16,36},{20,32},{24,44},{28,40},{32,2... | collective-permute-start | bytes 6291464 | tf_op jit(solution)/shard_map/cond/branch_13_fun/ppermute | solution.py:542
  103.0 85.1 %pull.29 = bf16[112,128,256]{2,1,0:T(8,128)(2,1)} custom-call(s32[1024]{0:T(1024)S(1)} %get-tuple-element.141.block_ids, bf16[8,16,128,256]{3,2,1,0:T(8,128)(2,1)} %get-tuple-element.142.hist), custom_call_target="tpu_custom_call" | custom-call | bytes 268435456 | tf_op jit(solution)/shard_map/cond/branch_13_fun/pull/pallas_call | solution.py:495
  188.1 4.8 %collective-permute-done.12 = bf16[4,1024,256]{2,1,0:T(8,128)(2,1)} collective-permute-done((bf16[4,1024,256]{2,1,0:T(8,128)(2,1)S(1)}, bf16[4,1024,256]{2,1,0:T(8,128)(2,1)}, u32[]{:S(2)}, u32[]{:S(2)}) %collective-permute-start.12) | collective-permute-done | bytes 2097184 | tf_op jit(solution)/shard_map/cond/branch_13_fun/ppermute | solution.py:542
  192.9 0.0 copy-done
  192.9 0.0 copy-done.1
  192.9 0.0 copy-done.2
  192.9 54.7 %layer.1 = bf16[4096,256]{1,0:T(8,128)(2,1)S(1)} custom-call(s32[8,32]{1,0:T(8,128)S(1)} %copy-done.1, bf16[32,128,256]{2,1,0:T(8,128)(2,1)} %bitcast.18, bf16[32,128,256]{2,1,0:T(8,128)(2,1)} %bitcast.9.refs_2_, bf16[16,128,256]{2,1,0:T(8,128)(2,1)S(1)} %bitcast.14, bf16[112,128,256]{2,1,0:T(8,128)(2,1)} %get-tuple-element.163.refs_4_, ...), custom_call_target="tpu_custom_call" | custom-call | tf_op jit(solution)/shard_map/layer/pallas_call | solution.py:160
  247.7 1.3 copy.46
Async XLA Ops:
  98.4 94.5 %copy-start = (bf16[8,2,128,256]{3,2,1,0:T(8,128)(2,1)S(1)}, bf16[8,2,128,256]{3,2,1,0:T(8,128)(2,1)}, u32[]{:S(2)}) copy-start(bf16[8,2,128,256]{3,2,1,0:T(8,128)(2,1)} %get-tuple-element.162) | copy-start | bytes 3145732
  98.4 94.5 %copy-start.1 = (s32[8,32]{1,0:T(8,128)S(1)}, s32[8,32]{1,0:T(8,128)}, u32[]{:S(2)}) copy-start(s32[8,32]{1,0:T(8,128)} %get-tuple-element.157.refs_0_) | copy-start | bytes 3076
  98.4 94.5 %copy-start.2 = (f32[256]{0:T(256)S(1)}, f32[256]{0:T(256)}, u32[]{:S(2)}) copy-start(f32[256]{0:T(256)} %param.33) | copy-start | bytes 3076
  98.6 94.3 %collective-permute-start.12 = (bf16[4,1024,256]{2,1,0:T(8,128)(2,1)S(1)}, bf16[4,1024,256]{2,1,0:T(8,128)(2,1)}, u32[]{:S(2)}, u32[]{:S(2)}) collective-permute-start(bf16[4,1024,256]{2,1,0:T(8,128)(2,1)S(1)} %get-tuple-element.140), channel_id=1, source_target_pairs={{0,52},{4,48},{8,60},{12,56},{16,36},{20,32},{24,44},{28,40},{32,2... | collective-permute-start | bytes 6291464 | tf_op jit(solution)/shard_map/cond/branch_13_fun/ppermute | solution.py:542
